TPU v7x, 256 devices: a whole 4x4x8 slice. The times are simulated.
256 devices in a mesh: atoms: 32 (over x_lo, z, core), beads: 8 (over x_hi, y).
Axes of the slice: x: 4 (x_hi: 2, x_lo: 2; x = x_hi * 2 + x_lo), y: 4, z: 8, core: 2. Of those that a mesh axis runs over, the one named last changes fastest.
Arguments:
- positions: float32 [32, 3, 4096], P('beads', None, 'atoms'), may hold values from 0 to 1
- velocities: float32 [32, 3, 4096], P('beads', None, 'atoms'), may hold values from -3 to 3
- charges_in: float32 [32, 4096], P('beads', 'atoms'), may hold values from -3 to 3
- species: int32 [4096], P('atoms'), may hold values from 0 to 7
- neighbors: int32 [8, 4096], P(None, 'atoms'), may hold values from -32 to 32
- k_index: int32 [3, 2048], replicated, may hold values from -8 to 8
- kernel: float32 [2048], replicated, may hold values from 0.1 to 1
- chi_table: float32 [8], replicated, may hold values from -2 to 2
- hard_table: float32 [8], replicated, may hold values from 1 to 4
- bond_table: float32 [8], replicated, may hold values from 0.2 to 0.8
- mass_table: float32 [8], replicated, may hold values from 1 to 8
Outputs:
- new_positions: float32 [32, 3, 4096], P('beads', None, 'atoms')
- new_velocities: float32 [32, 3, 4096], P('beads', None, 'atoms')
- charges: float32 [32, 4096], P('beads', 'atoms')
Inputs may be any that keep to these rules, and one draw needn't show every extreme that they name: species index the tables. `neighbors`: neighbour offsets count in atom order, cyclically over 4096 atoms.
All inputs are finite; a program needn't handle non-finite values.
Results may differ from a plain program's by a relative error of at most 0.00021.
Values sent between devices are 32-bit elements; how exact they have to be, the bound alone decides.
A program may use at most 64 MiB of HBM per device.

v0:
```python
import math

import jax
import jax.numpy as jnp
from jax import lax
from jax.sharding import PartitionSpec as P

KVEC = 2048
QITERS = 2
RIM = 32
SPECIES = 8


two_pi = 2.0 * math.pi
ewald_gain = 4.0
mixing = 0.5
spring_rate = 0.5
time_step = 0.05
HIGH = lax.Precision.HIGHEST


def extended(block, sides, width):
    for axis, dim in sides:
        count = lax.axis_size(axis)
        forward = [(i, i + 1) for i in range(count - 1)]
        forward.append((count - 1, 0))
        backward = [(target, source) for source, target in forward]
        low = lax.ppermute(
            lax.slice_in_dim(block, block.shape[dim] - width, None, axis=dim), axis, forward
        )
        high = lax.ppermute(lax.slice_in_dim(block, 0, width, axis=dim), axis, backward)
        block = jnp.concatenate([low, block, high], axis=dim)
    return block


def phase_tables(positions, nblock):
    angle = two_pi * (
        positions[:, 0, :, None] * nblock[0]
        + positions[:, 1, :, None] * nblock[1]
        + positions[:, 2, :, None] * nblock[2]
    )
    return (jnp.cos(angle), jnp.sin(angle))


def unblock(stacked):
    blocks, beads_here, parts, width = stacked.shape
    return stacked.transpose(1, 2, 0, 3).reshape(beads_here, parts, blocks * width)


def to_blocks(pair, blocks):
    beads_here, parts, total = pair.shape
    return pair.reshape(beads_here, parts, blocks, total // blocks).transpose(2, 0, 1, 3)


def local_factors(positions, charge, wave_blocks):

    def local_visit(unused, nblock):
        cosine, sine_part = phase_tables(positions, nblock)
        real_part = jnp.einsum("ba,bak->bk", charge, cosine, precision=HIGH)
        imag_part = jnp.einsum("ba,bak->bk", charge, sine_part, precision=HIGH)
        pair = jnp.stack([real_part, imag_part], 1)
        return (unused, pair)

    unused, stacked = lax.scan(local_visit, None, wave_blocks)
    return unblock(stacked)


def potential_sum(positions, pair, wave_blocks, kernel_blocks):
    coeff_blocks = to_blocks(pair, wave_blocks.shape[0]) * kernel_blocks[:, None, None, :]

    def potential_visit(accum, inputs):
        nblock, cblock = inputs
        cosine, sine_part = phase_tables(positions, nblock)
        accum = accum + jnp.einsum("bak,bk->ba", cosine, cblock[:, 0], precision=HIGH)
        return (accum + jnp.einsum("bak,bk->ba", sine_part, cblock[:, 1], precision=HIGH), None)

    start = jnp.zeros((positions.shape[0], positions.shape[2]), jnp.float32)
    result, unused = lax.scan(potential_visit, start, (wave_blocks, coeff_blocks))
    return result


def force_sum(positions, pair, wave_blocks, kernel_blocks):
    coeff_blocks = to_blocks(pair, wave_blocks.shape[0]) * kernel_blocks[:, None, None, :]

    def force_visit(accum, inputs):
        nblock, cblock = inputs
        cosine, sine_part = phase_tables(positions, nblock)
        mixed = sine_part * cblock[:, 0][:, None, :] - cosine * cblock[:, 1][:, None, :]
        return (accum + jnp.einsum("bak,dk->bda", mixed, nblock, precision=HIGH), None)

    result, unused = lax.scan(
        force_visit, jnp.zeros(positions.shape, jnp.float32), (wave_blocks, coeff_blocks)
    )
    return result


def summed_factors(positions, charge, wave_blocks):
    return lax.psum(local_factors(positions, charge, wave_blocks), "atoms")


def body(
    positions,
    velocities,
    charges_in,
    species,
    neighbors,
    k_index,
    kernel,
    chi_table,
    hard_table,
    bond_table,
    mass_table,
):
    atom_here = positions.shape[2]
    atom_count = atom_here * lax.axis_size("atoms")
    ewald_scale = ewald_gain / math.sqrt(KVEC * atom_count)
    width = min(256, KVEC)
    blocks = KVEC // width
    wave = k_index.astype(jnp.float32)
    wave_blocks = wave.reshape(3, blocks, width).transpose(1, 0, 2)
    kernel_blocks = kernel.reshape(blocks, width)
    onehot = (species[None, :] == jnp.arange(SPECIES, dtype=jnp.int32)[:, None]).astype(jnp.float32)

    def lookup(table):
        return jnp.sum(table[:, None] * onehot, 0)

    electroneg = lookup(chi_table)
    hardness = lookup(hard_table)
    bond_term = lookup(bond_table)
    atom_mass = lookup(mass_table)
    neighbour_index = jnp.arange(atom_here, dtype=jnp.int32)[None, :] + RIM + neighbors
    charge = charges_in
    for rounds in range(QITERS):
        pair = summed_factors(positions, charge, wave_blocks)
        potential = ewald_scale * potential_sum(positions, pair, wave_blocks, kernel_blocks)
        weighted = bond_term[None, :] * charge
        padded = extended(weighted, (("atoms", 1),), RIM)
        neighbour_sum = jnp.sum(padded[:, neighbour_index], 1)
        relaxed = (1.0 - mixing) * charge + mixing * (
            -(electroneg + potential + bond_term * neighbour_sum) / hardness
        )
        charge_sum = lax.psum(jnp.sum(relaxed, 1), "atoms")
        charge = relaxed - (charge_sum / atom_count)[:, None]
    pair = summed_factors(positions, charge, wave_blocks)
    ewald_force = (
        two_pi
        * ewald_scale
        * charge[:, None, :]
        * force_sum(positions, pair, wave_blocks, kernel_blocks)
    )
    padded_beads = extended(positions, (("beads", 0),), 1)
    laplace = 2.0 * positions - padded_beads[:-2] - padded_beads[2:]
    acceleration = ewald_force / atom_mass[None, None, :] - spring_rate * laplace
    new_velocities = velocities + time_step * acceleration
    new_positions = positions + time_step * new_velocities
    return (new_positions, new_velocities, charge)


def solution(mesh):
    return jax.shard_map(
        body,
        mesh=mesh,
        in_specs=(
            P("beads", None, "atoms"),
            P("beads", None, "atoms"),
            P("beads", "atoms"),
            P("atoms"),
            P(None, "atoms"),
            P(),
            P(),
            P(),
            P(),
            P(),
            P(),
        ),
        out_specs=(P("beads", None, "atoms"), P("beads", None, "atoms"), P("beads", "atoms")),
        check_vma=False,
    )
```

profile of v0, /device:TPU:1, one launch (start us, length us, event | category | flops | bytes accessed | tf_op | source)
XLA Modules:
  0.0 943.3 jit_solution(12425092056688733907)
XLA Ops:
  8.1 3.0 collective-permute-start
  12.9 40.7 %while.63 = (s32[]{:T(128)}, f32[8,4,2,256]{3,1,2,0:T(4,128)S(1)}, f32[4,3,128]{2,0,1:T(4,128)S(1)}, f32[8,3,256]{2,1,0:T(4,128)S(1)}, f32[4,128]{1,0:T(4,128)S(1)}, /*index=5*/s32[]{:T(128)}, s32[]{:T(128)}, s32[]{}, s32[]{}) while((s32[]{:T(128)}, f32[8,4,2,256]{3,1,2,0:T(4,128)S(1)}, f32[4,3,128]{2,0,1:T(4,128)S(1)}, ...), condition=%wide.region_2.0_spmd, body=%wide.region_1.0_spmd.sunk | while | flops 4720644 | bytes 114821 | solution.py:64
  15.4 2.5 fusion.184
  20.5 2.5 fusion.184
  25.6 2.5 fusion.184
  30.7 2.5 fusion.184
  35.8 2.5 fusion.184
  40.9 2.5 fusion.184
  46.0 2.5 fusion.184
  55.3 2.8 gather_fusion
  58.2 192.6 %all-reduce.4.cloned.1.call-done = f32[4,2,8,256]{3,0,1,2:T(4,128)} async-done(((f32[4,2,8,256]{3,0,1,2:T(4,128)}), f32[4,2,8,256]{3,0,1,2:T(4,128)}) %all-reduce.4.cloned.1.call-update) | async-done | bytes 65552 | tf_op jit(solution)/shard_map/psum | solution.py:98
  251.6 39.9 %while.66 = (s32[]{:T(128)}, f32[4,128]{1,0:T(4,128)S(1)}, f32[4,3,128]{2,0,1:T(4,128)S(1)}, f32[8,3,256]{2,1,0:T(4,128)S(1)}, f32[8,4,2,256]{3,1,2,0:T(4,128)S(1)}, /*index=5*/s32[]{:T(128)}, s32[]{:T(128)}, s32[]{}, s32[]{}) while((s32[]{:T(128)}, f32[4,128]{1,0:T(4,128)S(1)}, f32[4,3,128]{2,0,1:T(4,128)S(1)}, ...), condition=%wide.region_5.6_spmd.clone, body=%wide.region_4.5_spmd.clone.sunk | while | flops 4720133 | bytes 90255 | solution.py:78
  291.7 54.3 %psum.36 = f32[4]{0:T(128)S(1)} all-reduce(f32[4]{0:T(128)S(1)} %get-tuple-element.386), channel_id=1, replica_groups=mesh['atoms'=32,'beads'=8] {'atoms'}, use_global_device_ids=true, to_apply=%region_10.11 | all-reduce | flops 4 | bytes 32 | tf_op jit(solution)/shard_map/psum | solution.py:142
  348.0 40.7 %while.64 = (s32[]{:T(128)}, f32[8,4,2,256]{3,1,2,0:T(4,128)S(1)}, f32[4,3,128]{2,0,1:T(4,128)S(1)}, f32[8,3,256]{2,1,0:T(4,128)S(1)}, f32[4,128]{1,0:T(4,128)S(1)}, /*index=5*/s32[]{:T(128)}, s32[]{:T(128)}, s32[]{}, s32[]{}) while((s32[]{:T(128)}, f32[8,4,2,256]{3,1,2,0:T(4,128)S(1)}, f32[4,3,128]{2,0,1:T(4,128)S(1)}, ...), condition=%wide.region_12.13_spmd, body=%wide.region_11.12_spmd.sunk | while | flops 4720644 | bytes 114821 | solution.py:64
  389.6 2.8 gather_fusion.1
  392.6 189.6 %all-reduce.6.cloned.1.call-done = f32[4,2,8,256]{3,0,1,2:T(4,128)} async-done(((f32[4,2,8,256]{3,0,1,2:T(4,128)}), f32[4,2,8,256]{3,0,1,2:T(4,128)}) %all-reduce.6.cloned.1.call-update) | async-done | bytes 65552 | tf_op jit(solution)/shard_map/psum | solution.py:98
  583.0 39.9 %while.67 = (s32[]{:T(128)}, f32[4,128]{1,0:T(4,128)S(1)}, f32[4,3,128]{2,0,1:T(4,128)S(1)}, f32[8,3,256]{2,1,0:T(4,128)S(1)}, f32[8,4,2,256]{3,1,2,0:T(4,128)S(1)}, /*index=5*/s32[]{:T(128)}, s32[]{:T(128)}, s32[]{}, s32[]{}) while((s32[]{:T(128)}, f32[4,128]{1,0:T(4,128)S(1)}, f32[4,3,128]{2,0,1:T(4,128)S(1)}, ...), condition=%wide.region_15.16_spmd.clone, body=%wide.region_14.15_spmd.clone.sunk | while | flops 4720133 | bytes 90255 | solution.py:78
  623.1 54.3 %psum.38 = f32[4]{0:T(128)S(1)} all-reduce(f32[4]{0:T(128)S(1)} %get-tuple-element.382), channel_id=1, replica_groups=mesh['atoms'=32,'beads'=8] {'atoms'}, use_global_device_ids=true, to_apply=%region_18.19 | all-reduce | flops 4 | bytes 32 | tf_op jit(solution)/shard_map/psum | solution.py:142
  677.5 40.8 %while.65 = (s32[]{:T(128)}, f32[8,4,2,256]{3,1,2,0:T(4,128)S(1)}, f32[4,3,128]{2,0,1:T(4,128)S(1)}, f32[8,3,256]{2,1,0:T(4,128)S(1)}, f32[4,128]{1,0:T(4,128)S(1)}, /*index=5*/s32[]{:T(128)}, s32[]{:T(128)}, s32[]{}, s32[]{}) while((s32[]{:T(128)}, f32[8,4,2,256]{3,1,2,0:T(4,128)S(1)}, f32[4,3,128]{2,0,1:T(4,128)S(1)}, ...), condition=%wide.region_20.21_spmd, body=%wide.region_19.20_spmd.sunk | while | flops 4720644 | bytes 114821 | solution.py:64
  680.0 2.5 fusion.196
  685.1 2.5 fusion.196
  720.0 4.1 collective-permute-start.5
  724.1 185.2 %all-reduce.8.cloned.1.call-done = f32[4,2,8,256]{3,0,1,2:T(4,128)} async-done(((f32[4,2,8,256]{3,0,1,2:T(4,128)}), f32[4,2,8,256]{3,0,1,2:T(4,128)}) %all-reduce.8.cloned.1.call-update) | async-done | bytes 65552 | tf_op jit(solution)/shard_map/psum | solution.py:98
  910.2 25.9 %while.68 = (s32[]{:T(128)}, f32[4,3,128]{2,1,0:T(4,128)S(1)}, f32[8,3,256]{2,1,0:T(4,128)S(1)}, f32[4,3,128]{2,0,1:T(4,128)S(1)}, f32[8,4,2,256]{3,1,2,0:T(4,128)S(1)}, /*index=5*/s32[]{:T(128)}, s32[]{:T(128)}, s32[]{}, s32[]{}) while((s32[]{:T(128)}, f32[4,3,128]{2,1,0:T(4,128)S(1)}, f32[8,3,256]{2,1,0:T(4,128)S(1)}, ...), condition=%wide.region_23.24_spmd.clone, body=%wide.region_22.23_spmd.clone.sunk | while | flops 5901317 | bytes 87187 | solution.py:91
  910.3 3.1 fusion.210
  913.5 3.1 fusion.210
  916.8 3.1 fusion.210
  920.0 3.1 fusion.210
  923.3 3.1 fusion.210
  926.5 3.1 fusion.210
  929.7 3.1 fusion.210
  933.0 3.1 fusion.210
  (442 shorter events, 190.7 us)
Async XLA Ops:
  7.2 243.6 %all-reduce.4.cloned.1.call-start = ((), (), s32[]{:S(2)}) async-start(), calls=%async_computation | async-start | bytes 131072 | tf_op jit(solution)/shard_map/psum | solution.py:98
  7.2 0.8 copy-start.4
  8.1 46.9 %collective-permute-start = (f32[4,32]{1,0:T(4,128)S(1)}, f32[4,32]{1,0:T(4,128)S(1)}, u32[]{:S(2)}, u32[]{:S(2)}) collective-permute-start(f32[4,32]{1,0:T(4,128)S(1)} %get-tuple-element.430), channel_id=1, source_target_pairs={{0,8},{8,16},{16,24},{24,32},{32,40},{40,48},{48,56},{56,64},{64,7... | collective-permute-start | bytes 1544 | tf_op jit(solution)/shard_map/ppermute | solution.py:28
  11.2 43.9 %collective-permute-start.1 = (f32[4,32]{1,0:T(4,128)S(1)}, f32[4,32]{1,0:T(4,128)S(1)}, u32[]{:S(2)}, u32[]{:S(2)}) collective-permute-start(f32[4,32]{1,0:T(4,128)S(1)} %get-tuple-element.431), channel_id=1, source_target_pairs={{8,0},{16,8},{24,16},{32,24},{40,32},{48,40},{56,48},{64,56},{72,6... | collective-permute-start | bytes 1544 | tf_op jit(solution)/shard_map/ppermute | solution.py:31
  12.2 0.7 copy-start
  53.6 0.6 copy-start.2
  53.6 0.7 copy-start.7
  54.3 527.9 %all-reduce.6.cloned.1.call-start = ((), (), s32[]{:S(2)}) async-start(), calls=%async_computation.1 | async-start | bytes 131072 | tf_op jit(solution)/shard_map/psum | solution.py:98
  54.4 0.7 copy-start.5
  346.1 43.3 %collective-permute-start.2 = (f32[4,32]{1,0:T(4,128)S(1)}, f32[4,32]{1,0:T(4,128)S(1)}, u32[]{:S(2)}, u32[]{:S(2)}) collective-permute-start(f32[4,32]{1,0:T(4,128)S(1)} %get-tuple-element.428), channel_id=1, source_target_pairs={{0,8},{8,16},{16,24},{24,32},{32,40},{40,48},{48,56},{56,64},{64,7... | collective-permute-start | bytes 1544 | tf_op jit(solution)/shard_map/ppermute | solution.py:28
  346.1 43.3 %collective-permute-start.3 = (f32[4,32]{1,0:T(4,128)S(1)}, f32[4,32]{1,0:T(4,128)S(1)}, u32[]{:S(2)}, u32[]{:S(2)}) collective-permute-start(f32[4,32]{1,0:T(4,128)S(1)} %get-tuple-element.429), channel_id=1, source_target_pairs={{8,0},{16,8},{24,16},{32,24},{40,32},{48,40},{56,48},{64,56},{72,6... | collective-permute-start | bytes 1544 | tf_op jit(solution)/shard_map/ppermute | solution.py:31
  388.7 0.6 copy-start.3
  389.4 520.0 %all-reduce.8.cloned.1.call-start = ((), (), s32[]{:S(2)}) async-start(), calls=%async_computation.2 | async-start | bytes 131072 | tf_op jit(solution)/shard_map/psum | solution.py:98
  718.3 0.6 copy-start.8
  718.3 0.6 copy-start.1
  719.0 217.2 %collective-permute-start.4 = (f32[1,3,128]{2,0,1:T(1,128)S(1)}, f32[1,3,128]{2,0,1:T(1,128)S(1)}, u32[]{:S(2)}, u32[]{:S(2)}) collective-permute-start(f32[1,3,128]{2,0,1:T(1,128)S(1)} %get-tuple-element.426), channel_id=1, source_target_pairs={{0,1},{1,2},{2,3},{3,4},{4,5},{5,6},{6,7},{7,0},{8,9},{9,10},{10,1... | collective-permute-start | bytes 4616 | tf_op jit(solution)/shard_map/ppermute | solution.py:28
  720.0 216.2 %collective-permute-start.5 = (f32[1,3,128]{2,0,1:T(1,128)S(1)}, f32[1,3,128]{2,0,1:T(1,128)S(1)}, u32[]{:S(2)}, u32[]{:S(2)}) collective-permute-start(f32[1,3,128]{2,0,1:T(1,128)S(1)} %get-tuple-element.427), channel_id=1, source_target_pairs={{1,0},{2,1},{3,2},{4,3},{5,4},{6,5},{7,6},{0,7},{9,8},{10,9},{11,1... | collective-permute-start | bytes 4616 | tf_op jit(solution)/shard_map/ppermute | solution.py:31
  910.2 26.0 %copy-start.6 = (f32[4,3,128]{2,0,1:T(4,128)S(1)}, f32[4,3,128]{2,0,1:T(4,128)}, u32[]{:S(2)}) copy-start(f32[4,3,128]{2,0,1:T(4,128)} %param.24) | copy-start | bytes 18436
Sparse Core Ops, SparseCore 0:
  54.4 196.3 all-reduce.3
  389.5 192.6 all-reduce.5
  719.1 190.2 all-reduce.7
where the time goes:
time: 945 us; the launch traced here: 943 us
  waiting for transfers between devices  567 us (60%)
  matrix products  223 us (24%)
  blocking collectives  109 us (12%)
  between operations  14.1 us (1%)
  local copies, waits for them, and re-layouts  11.7 us (1%)
  starting transfers between devices  10.4 us (1%)
    psum x3, waiting for transfers between devices, summed_factors(): return lax.psum(local_factors(positions, charge, wave_blocks), 'atoms')  567 us
    psum x2, blocking collectives, body(): charge_sum = lax.psum(jnp.sum(relaxed, 1), 'atoms')  109 us
    dot_general x24, matrix products, local_visit(): imag_part = jnp.einsum('ba,bak->bk', charge, sine_part, precision=HIGH)  59.9 us
    dot_general x24, matrix products, local_visit(): real_part = jnp.einsum('ba,bak->bk', charge, cosine, precision=HIGH)  59.5 us
    dot_general x16, matrix products, potential_visit(): jnp.einsum('bak,bk->ba', sine_part, cblock[:, 1], precision=HIGH)  39.5 us
    dot_general x16, matrix products, potential_visit(): jnp.einsum('bak,bk->ba', cosine, cblock[:, 0], precision=HIGH)  38.8 us
    dot_general x8, matrix products, force_visit(): jnp.einsum('bak,dk->bda', mixed, nblock, precision=HIGH)  25.1 us
  transfers between devices with their start and end apart: 9, of which 3 were waited for; matrix products, arithmetic and copies ran while one was open for 12% of the time, Pallas kernels for 0%

commit v1 on v0

v1 whole, which is shorter than its diff:
```python
import math

import jax
import jax.numpy as jnp
from jax import lax
from jax.experimental import pallas as pl
from jax.experimental.pallas import tpu as pltpu
from jax.sharding import PartitionSpec as P

KVEC = 2048
SPECIES = 8
ATOMS = 4096
GROUP = 32
BEAD_AXIS = 8
BLOCK = 128
SLOTS = 16
HALF = SLOTS * BLOCK
TILES = 38
ROWS = TILES * 8
EXROWS = ROWS + 8

two_pi = 2.0 * math.pi
ewald_scale = 4.0 / math.sqrt(KVEC * ATOMS)
time_step = 0.05
spring_rate = 0.5

COS = (1.0, -19.7392087, 64.9393891, -85.4566583, 60.2421313, -26.4046682, 7.80013144, -1.45311232)
SIN = (6.2831853, -41.3417004, 81.6051314, -76.7030154, 42.025927, -14.8998467, 3.2381375)

MESH = pl.DeviceIdType.MESH
NT = (((1,), (1,)), ((), ()))
f32 = jnp.float32
bf16 = jnp.bfloat16


def horner(coeffs, s):
    total = coeffs[-1] * s + coeffs[-2]
    for value in coeffs[-3::-1]:
        total = total * s + value
    return total


def harmonics(row):
    n = lax.broadcasted_iota(jnp.int32, (8, row.shape[1]), 0).astype(f32) + 1.0
    turns = n * row
    r = turns - jnp.floor(turns + 0.5)
    s = r * r
    return horner(COS, s), r * horner(SIN, s)


def split(x):
    high = x.astype(bf16)
    return high, x - high.astype(f32)


def tile(x, t):
    return x[8 * t : 8 * t + 8, :]


def flip(x):
    lane = lax.broadcasted_iota(jnp.int32, x.shape, 1)
    return jnp.where(lane < 16, pltpu.roll(x, 112, 1), pltpu.roll(x, 16, 1))


def core_tile(ta, tb, a):
    return 16 * ta + 8 * tb + a


def expand(coeff):
    high, low = split(coeff)
    return (high.astype(f32) + pltpu.roll(low, 32, 1) + pltpu.roll(high.astype(f32), 64, 1)).astype(bf16)


def kernel_body(
    pos_ref,
    vel_ref,
    chg_ref,
    spec_ref,
    nbr_ref,
    k_ref,
    kern_ref,
    chi_ref,
    hard_ref,
    bond_ref,
    mass_ref,
    npos_ref,
    nvel_ref,
    nchg_ref,
    send_s,
    buf,
    nbuf,
    utab,
    uhi,
    ulo,
    wtab,
    wst,
    acols,
    etab,
    ex_s,
    ex_r,
    factor,
    coef,
    lhs,
    phi_s,
    near_s,
    nbond_s,
    ext_s,
    fsend,
    frecv,
    halo,
    s_sem,
    r_sem,
    ns_sem,
    nr_sem,
    xs_sem,
    xr_sem,
    fs_sem,
    fr_sem,
    hs_sem,
    hr_sem,
):
    me = lax.axis_index("atoms")
    bead = lax.axis_index("beads")
    x_lo = me // 16
    z = (me // 2) % 8
    core = me % 2
    quad = z // 2
    partner = x_lo * 16 + z * 2 + (1 - core)
    next_bead = (bead + 1) % BEAD_AXIS
    prev_bead = (bead + BEAD_AXIS - 1) % BEAD_AXIS

    barrier = pltpu.get_barrier_semaphore()

    def greet(k, carry):
        pl.semaphore_signal(barrier, inc=1, device_id={"atoms": (me + k) % GROUP}, device_id_type=MESH)
        return carry

    lax.fori_loop(1, GROUP, greet, 0)
    for other in (next_bead, prev_bead):
        pl.semaphore_signal(barrier, inc=1, device_id={"beads": other}, device_id_type=MESH)

    species = spec_ref[...]

    def lookup(table):
        total = jnp.zeros((1, BLOCK), f32)
        for s in range(SPECIES):
            total = jnp.where(species == s, table[0, s], total)
        return total

    chi_row, hard_row, bond_row, mass_row = (lookup(t) for t in (chi_ref, hard_ref, bond_ref, mass_ref))
    for b in range(4):
        send_s[b, 0:3, :] = pos_ref[b]
        send_s[b, 3:4, :] = chg_ref[b : b + 1, :]
        send_s[b, 4:5, :] = chi_row
        send_s[b, 5:6, :] = hard_row
        send_s[b, 6:7, :] = bond_row
        send_s[b, 7:8, :] = bond_row

    pl.semaphore_wait(barrier, GROUP + 1)

    slot = z * 2 + core

    def far_dest(b, o):
        return (b >> 1) * 16 + (2 * ((quad + o) % 4) + (b & 1)) * 2 + x_lo

    def data_copy(b, o, dest):
        return pltpu.make_async_remote_copy(
            send_s.at[b], buf.at[slot], s_sem.at[4 * o + b], r_sem.at[slot], device_id={"atoms": dest}, device_id_type=MESH
        )

    def nbr_copy(b, o, dest):
        return pltpu.make_async_remote_copy(
            nbr_ref, nbuf.at[slot], ns_sem.at[4 * o + b], nr_sem.at[slot], device_id={"atoms": dest}, device_id_type=MESH
        )

    order = [(b, o) for o in (2, 1, 3, 0) for b in range(4)]
    for make, source, store, sem in (
        (data_copy, lambda b: send_s.at[b], buf, r_sem),
        (nbr_copy, lambda b: nbr_ref, nbuf, nr_sem),
    ):
        for b, o in order:
            dest = far_dest(b, o)
            if o:
                make(b, o, dest).start()
            else:

                @pl.when(dest != me)
                def _():
                    make(b, o, dest).start()

                @pl.when(dest == me)
                def _():
                    pltpu.make_async_copy(source(b), store.at[slot], sem.at[slot]).start()

    to_next = pltpu.make_async_remote_copy(
        pos_ref.at[3], halo.at[0], hs_sem.at[0], hr_sem.at[0], device_id={"beads": next_bead}, device_id_type=MESH
    )
    to_prev = pltpu.make_async_remote_copy(
        pos_ref.at[0], halo.at[1], hs_sem.at[1], hr_sem.at[1], device_id={"beads": prev_bead}, device_id_type=MESH
    )
    to_next.start()
    to_prev.start()

    nx, ny, nz = (k_ref[d : d + 1, :] for d in range(3))
    ax, ay, az = jnp.abs(nx), jnp.abs(ny), jnp.abs(nz)
    code = jnp.where(
        ax > 0,
        jnp.where(ay > 0, 8 * (ax - 1) + ay - 1, 72 + ax - 1),
        jnp.where(ay > 0, 64 + ay - 1, 80),
    )
    row_hot = jnp.where(lax.broadcasted_iota(jnp.int32, (96, KVEC), 0) == code, 1.0, 0.0).astype(bf16)
    lane_code = jnp.where(az > 0, az - 1, 8)
    lane_hot = lax.broadcasted_iota(jnp.int32, (16, KVEC), 0) == lane_code
    sx, sy, sz = (jnp.where(n < 0, -1.0, 1.0) for n in (nx, ny, nz))
    weight = kern_ref[...]
    parts = [[], []]
    for j, sign in enumerate((None, -sy * sz, -sx * sz, -sx * sy)):
        value = weight if sign is None else weight * sign
        high = value.astype(bf16).astype(f32)
        for part, piece in zip(parts, (high, value - high)):
            block = jnp.where(lane_hot, piece, 0.0)
            part += [block, -block if j in (1, 2) else block]
    grid = None
    for part in parts:
        term = lax.dot_general(row_hot, jnp.concatenate(part, 0).astype(bf16), NT, preferred_element_type=f32)
        grid = term if grid is None else grid + term
    lane = lax.broadcasted_iota(jnp.int32, (96, 128), 1)
    for j in range(4):
        moved = grid if j == 0 else pltpu.roll(grid, 128 - 32 * j, 1)
        etab[j] = jnp.where(lane < 32, moved, 0.0)

    factor[...] = jnp.zeros((ROWS, 128), f32)
    first = jnp.where(lax.broadcasted_iota(jnp.int32, (8, 512), 0) == 0, 1.0, 0.0)
    zero8 = jnp.zeros((8, 512), f32)

    def arrive(step, carry):
        offset = jnp.where(step == 0, 0, jnp.where(step == 1, 1, jnp.where(step == 2, 3, 2)))
        base = ((quad + offset) % 4) * 4
        for m in range(4):
            pltpu.make_async_remote_copy(
                send_s.at[0],
                buf.at[base + m],
                s_sem.at[0],
                r_sem.at[base + m],
                device_id={"atoms": partner},
                device_id_type=MESH,
            ).wait_recv()
        rows = [jnp.concatenate([buf[base + m, r : r + 1, :] for m in range(4)], 1) for r in range(4)]
        at = pl.ds(pl.multiple_of(base * BLOCK, 512), 512)
        (cu, su), (cv, sv), (cw, sw) = (harmonics(rows[d]) for d in range(3))

        def put(t, low_tile, high_tile):
            both = jnp.concatenate([low_tile, high_tile], 0)
            utab[8 * t : 8 * t + 16, at] = both
            high, low = split(both)
            uhi[8 * t : 8 * t + 16, at] = high
            ulo[8 * t : 8 * t + 16, at] = low.astype(bf16)

        for ta, u in ((0, cu), (1, su)):
            for tb, v in ((0, cv), (1, sv)):
                for a in range(0, 8, 2):
                    put(core_tile(ta, tb, a), u[a : a + 1, :] * v, u[a + 1 : a + 2, :] * v)
        put(32, cv, sv)
        put(34, cu, su)
        put(36, first, zero8)

        w = jnp.concatenate([cw, first, sw, zero8], 0)
        wtab[:, at] = w
        whi, wlo = split(w)
        wlo = wlo.astype(bf16)
        wst[0:32, at] = whi
        wst[32:64, at] = whi
        wst[64:96, at] = wlo
        wst[96:128, at] = jnp.zeros((32, 512), bf16)
        qhi, qlo = split(w * rows[3])
        a_block = jnp.concatenate([qhi, qlo.astype(bf16), whi, wlo], 0)
        acols[:, at] = a_block
        factor[...] += lax.dot_general(uhi[:, at], a_block, NT, preferred_element_type=f32) + lax.dot_general(
            ulo[:, at], a_block, NT, preferred_element_type=f32
        )
        return carry

    lax.fori_loop(0, 4, arrive, 0)

    charge = buf[:, 3, :]
    chi = buf[:, 4, :]
    inv_hard = 1.0 / buf[:, 5, :]
    bond = buf[:, 6, :]

    def start_exchange(r, weighted):
        ex_s[r, 0:ROWS, :] = factor[...]
        ends = jnp.concatenate(
            [weighted[0:1, :], weighted[15:16, :], bond[0:1, :], bond[15:16, :], jnp.zeros((4, 128), f32)], 0
        )
        ex_s[r, ROWS:EXROWS, :] = ends
        copy = pltpu.make_async_remote_copy(
            ex_s.at[r], ex_r.at[r], xs_sem.at[r], xr_sem.at[r], device_id={"atoms": partner}, device_id_type=MESH
        )
        copy.start()
        return copy

    def mix(r, centre):
        total = ex_s[r, 0:ROWS, :] + ex_r[r, 0:ROWS, :]
        total = total + pltpu.roll(total, 96, 1)
        mean = 0.0
        if centre:
            mean = total[8 * 36 : 8 * 36 + 1, 8:9] * (1.0 / ATOMS)
            total = total - mean * pltpu.roll(total, 64, 1)
        for ta in range(2):
            for tb in range(2):
                for a in range(8):
                    here = tile(total, core_tile(ta, tb, a))
                    both = tile(total, core_tile(1 - ta, 1 - tb, a))
                    over_b = flip(tile(total, core_tile(ta, 1 - tb, a)))
                    over_a = flip(tile(total, core_tile(1 - ta, tb, a)))
                    e = [etab[j, 8 * a : 8 * a + 8, :] for j in range(4)]
                    out = e[0] * here
                    out = out + e[3] * both if ta == tb else out - e[3] * both
                    out = out + e[1] * over_b if tb == 0 else out - e[1] * over_b
                    out = out + e[2] * over_a if ta == 0 else out - e[2] * over_a
                    t = core_tile(ta, tb, a)
                    coef[8 * t : 8 * t + 8, :] = out
        for first_tile, row, j in ((32, 64, 1), (34, 72, 2)):
            e0 = etab[0, row : row + 8, :]
            ej = etab[j, row : row + 8, :]
            c, s = tile(total, first_tile), tile(total, first_tile + 1)
            coef[8 * first_tile : 8 * first_tile + 8, :] = e0 * c + ej * flip(s)
            coef[8 * first_tile + 8 : 8 * first_tile + 16, :] = e0 * s - ej * flip(c)
        coef[8 * 36 : 8 * 37, :] = etab[0, 80:88, :] * tile(total, 36)
        coef[8 * 37 : 8 * 38, :] = jnp.zeros((8, 128), f32)
        return mean

    def potential():
        lhs[0:ROWS, :] = expand(coef[...])

        def visit(i, carry):
            at = pl.ds(pl.multiple_of(i * 256, 256), 256)
            fields = jnp.dot(lhs[0:ROWS, :], wst[:, at], preferred_element_type=f32)
            total = jnp.sum((fields * utab[:, at]).reshape(TILES, 8, 256), 0)
            row = jnp.sum(total, 0, keepdims=True)
            phi_s[pl.ds(2 * i, 1), :] = row[:, 0:128]
            phi_s[pl.ds(2 * i + 1, 1), :] = row[:, 128:256]
            return carry

        lax.fori_loop(0, SLOTS // 2, visit, 0)

    def near_sums(own, left, right, out):
        ext_s[0:1, :] = left
        ext_s[1:17, :] = own
        ext_s[17:18, :] = right
        lane_at = lax.broadcasted_iota(jnp.int32, (8, BLOCK), 1)

        def visit(j, carry):
            target = lane_at + nbuf[j]
            index = target & (BLOCK - 1)
            low, mid, high = (
                jnp.take_along_axis(
                    jnp.broadcast_to(ext_s[pl.ds(j + d, 1), :], (8, BLOCK)), index, axis=1, mode="promise_in_bounds"
                )
                for d in range(3)
            )
            got = jnp.where(target < 0, low, jnp.where(target >= BLOCK, high, mid))
            out[pl.ds(j, 1), :] = jnp.sum(got, 0, keepdims=True)
            return carry

        lax.fori_loop(0, SLOTS, visit, 0)

    def refactor(values):
        for j in range(SLOTS):
            at = slice(j * BLOCK, (j + 1) * BLOCK)
            qhi, qlo = split(wtab[:, at] * values[j : j + 1, :])
            acols[0:32, at] = qhi
            acols[32:64, at] = qlo.astype(bf16)
        factor[...] = lax.dot_general(uhi[...], acols[...], NT, preferred_element_type=f32) + lax.dot_general(
            ulo[...], acols[...], NT, preferred_element_type=f32
        )

    def relax(charge, near):
        potential_here = ewald_scale * phi_s[...]
        return 0.5 * charge + 0.5 * (-(chi + potential_here + bond * near) * inv_hard)

    weighted = bond * charge
    exchange = start_exchange(0, weighted)

    def wait_nbr(j, carry):
        pltpu.make_async_remote_copy(
            nbr_ref, nbuf.at[j], ns_sem.at[0], nr_sem.at[j], device_id={"atoms": partner}, device_id_type=MESH
        ).wait_recv()
        return carry

    lax.fori_loop(0, SLOTS, wait_nbr, 0)
    exchange.wait()
    ends = ex_r[0, ROWS:EXROWS, :]
    near_sums(bond, ends[3:4, :], ends[2:3, :], nbond_s)
    near_sums(weighted, ends[1:2, :], ends[0:1, :], near_s)
    mix(0, False)
    potential()
    relaxed = relax(charge, near_s[...])

    weighted = bond * relaxed
    refactor(relaxed)
    exchange = start_exchange(1, weighted)
    exchange.wait()
    ends = ex_r[1, ROWS:EXROWS, :]
    near_sums(weighted, ends[1:2, :], ends[0:1, :], near_s)
    mean = mix(1, True)
    potential()
    charge = relaxed - mean
    relaxed = relax(charge, near_s[...] - mean * nbond_s[...])

    refactor(relaxed)
    exchange = start_exchange(2, bond * relaxed)
    exchange.wait()
    mean = mix(2, True)
    near_s[...] = relaxed - mean

    lane = lax.broadcasted_iota(jnp.int32, (ROWS, 128), 1)
    number = jnp.where((lane & 15) < 8, (lane & 15) + 1, 0).astype(f32)
    slope = jnp.where(lane < 16, number, -number)
    whole = coef[...]
    lhs[0:ROWS, :] = expand(whole)
    lhs[ROWS : 2 * ROWS, :] = expand(jnp.where(lane < 32, flip(whole) * slope, 0.0))
    ones = lax.broadcasted_iota(jnp.int32, (8, 256), 0).astype(f32) + 1.0

    def force(i, carry):
        at = pl.ds(pl.multiple_of(quad * 512 + i * 256, 256), 256)
        fields = jnp.dot(lhs[...], wst[:, at], preferred_element_type=f32)
        basis = [utab[8 * t : 8 * t + 8, at] for t in range(37)]

        def plain(t):
            return fields[8 * t : 8 * t + 8, :]

        dz = basis[0] * fields[ROWS : ROWS + 8, :]
        for t in range(1, 37):
            dz = dz + basis[t] * fields[ROWS + 8 * t : ROWS + 8 * t + 8, :]
        dx = jnp.zeros((8, 256), f32)
        for a in range(8):
            term = jnp.zeros((8, 256), f32)
            for tb in range(2):
                c, s = core_tile(0, tb, a), core_tile(1, tb, a)
                term = term + basis[c] * plain(s) - basis[s] * plain(c)
            dx = dx + (a + 1.0) * term
        dx = dx + ones * (basis[34] * plain(35) - basis[35] * plain(34))
        dy = basis[32] * plain(33) - basis[33] * plain(32)
        for ta in range(2):
            for a in range(8):
                c, s = core_tile(ta, 0, a), core_tile(ta, 1, a)
                dy = dy + basis[c] * plain(s) - basis[s] * plain(c)
        dy = dy * ones
        dx, dy, dz = (jnp.sum(d, 0, keepdims=True) for d in (dx, dy, dz))
        for m in range(2):
            own = near_s[pl.ds(quad * 4 + 2 * i + m, 1), :]
            piece = slice(128 * m, 128 * m + 128)
            fsend[2 * i + m] = jnp.concatenate(
                [dx[:, piece], dy[:, piece], dz[:, piece], own, jnp.zeros((4, 128), f32)], 0
            )
        return carry

    lax.fori_loop(0, 2, force, 0)

    my_bead = 2 * x_lo + z % 2

    def force_copy(m):
        home = core * 16 + (2 * quad + (m >> 1)) * 2 + (m & 1)
        return home, pltpu.make_async_remote_copy(
            fsend.at[m], frecv.at[my_bead], fs_sem.at[m], fr_sem.at[my_bead], device_id={"atoms": home}, device_id_type=MESH
        )

    for m in range(4):
        home, copy = force_copy(m)

        @pl.when(home != me)
        def _():
            copy.start()

        @pl.when(home == me)
        def _():
            pltpu.make_async_copy(fsend.at[m], frecv.at[my_bead], fr_sem.at[my_bead]).start()

    for make in (data_copy, nbr_copy):
        for b, o in order:
            dest = far_dest(b, o)
            if o:
                make(b, o, dest).wait_send()
            else:

                @pl.when(dest != me)
                def _():
                    make(b, o, dest).wait_send()

    to_next.wait()
    to_prev.wait()
    inv_mass = 1.0 / mass_row
    for b in range(4):
        pltpu.make_async_remote_copy(
            fsend.at[0], frecv.at[b], fs_sem.at[0], fr_sem.at[b], device_id={"atoms": partner}, device_id_type=MESH
        ).wait_recv()
        got = frecv[b]
        charges = got[3:4, :]
        nchg_ref[b : b + 1, :] = charges
        ewald_force = (-two_pi * ewald_scale) * charges * got[0:3, :]
        here = pos_ref[b]
        before = halo[0] if b == 0 else pos_ref[b - 1]
        after = halo[1] if b == 3 else pos_ref[b + 1]
        laplace = 2.0 * here - before - after
        speed = vel_ref[b] + time_step * (ewald_force * inv_mass - spring_rate * laplace)
        nvel_ref[b] = speed
        npos_ref[b] = here + time_step * speed
    for m in range(4):
        home, copy = force_copy(m)

        @pl.when(home != me)
        def _():
            copy.wait_send()


def step(positions, velocities, charges_in, species, neighbors, k_index, kernel, chi, hard, bond, mass):
    vmem = pl.BlockSpec(memory_space=pltpu.VMEM)
    smem = pl.BlockSpec(memory_space=pltpu.SMEM)
    dma = pltpu.SemaphoreType.DMA
    return pl.pallas_call(
        kernel_body,
        out_shape=(
            jax.ShapeDtypeStruct(positions.shape, f32),
            jax.ShapeDtypeStruct(velocities.shape, f32),
            jax.ShapeDtypeStruct(charges_in.shape, f32),
        ),
        in_specs=[vmem] * 7 + [smem] * 4,
        out_specs=(vmem, vmem, vmem),
        scratch_shapes=[
            pltpu.VMEM((4, 8, 128), f32),
            pltpu.VMEM((SLOTS, 8, 128), f32),
            pltpu.VMEM((SLOTS, 8, 128), jnp.int32),
            pltpu.VMEM((ROWS, HALF), f32),
            pltpu.VMEM((ROWS, HALF), bf16),
            pltpu.VMEM((ROWS, HALF), bf16),
            pltpu.VMEM((32, HALF), f32),
            pltpu.VMEM((128, HALF), bf16),
            pltpu.VMEM((128, HALF), bf16),
            pltpu.VMEM((4, 96, 128), f32),
            pltpu.VMEM((3, EXROWS, 128), f32),
            pltpu.VMEM((3, EXROWS, 128), f32),
            pltpu.VMEM((ROWS, 128), f32),
            pltpu.VMEM((ROWS, 128), f32),
            pltpu.VMEM((2 * ROWS, 128), bf16),
            pltpu.VMEM((SLOTS, 128), f32),
            pltpu.VMEM((SLOTS, 128), f32),
            pltpu.VMEM((SLOTS, 128), f32),
            pltpu.VMEM((24, 128), f32),
            pltpu.VMEM((4, 8, 128), f32),
            pltpu.VMEM((4, 8, 128), f32),
            pltpu.VMEM((2, 3, 128), f32),
            dma((16,)),
            dma((16,)),
            dma((16,)),
            dma((16,)),
            dma((3,)),
            dma((3,)),
            dma((4,)),
            dma((4,)),
            dma((2,)),
            dma((2,)),
        ],
        compiler_params=pltpu.CompilerParams(collective_id=0, has_side_effects=True, vmem_limit_bytes=48 * 1024 * 1024),
        name="pimd_step",
    )(
        positions,
        velocities,
        charges_in,
        species.reshape(1, BLOCK),
        neighbors,
        k_index,
        kernel.reshape(1, KVEC),
        *(t.reshape(1, SPECIES) for t in (chi, hard, bond, mass)),
    )


def solution(mesh):
    return jax.shard_map(
        step,
        mesh=mesh,
        in_specs=(
            P("beads", None, "atoms"),
            P("beads", None, "atoms"),
            P("beads", "atoms"),
            P("atoms"),
            P(None, "atoms"),
            P(),
            P(),
            P(),
            P(),
            P(),
            P(),
        ),
        out_specs=(P("beads", None, "atoms"), P("beads", None, "atoms"), P("beads", "atoms")),
        check_vma=False,
    )
```

time: 945 us -> 42.8 us (0.05)
  waiting for transfers between devices: 567 us -> 0 us
  matrix products: 223 us -> 0 us
  blocking collectives: 109 us -> 0 us
  Pallas kernels: 0 us -> 36 us
  between operations: 14.1 us -> 0.69 us
  starting transfers between devices: 10.4 us -> 0 us
    psum x3 -> x0, waiting for transfers between devices: 567 us -> none  [summed_factors(): return lax.psum(local_factors(positions, charge, wave_blocks), 'atoms')]
    dot_general x88 -> x0, matrix products: 223 us -> none  [the longest x24 59.9 us: local_visit(): imag_part = jnp.einsum('ba,bak->bk', charge, sine_part, precision=HIGH)]
    psum x2 -> x0, blocking collectives: 109 us -> none  [body(): charge_sum = lax.psum(jnp.sum(relaxed, 1), 'atoms')]
    pallas_call x0 -> x1, Pallas kernels: none -> 36 us  [step(): pl.pallas_call(kernel_body, out_shape=(jax.ShapeDtypeStruct(positions.sha...]
    ppermute x6 -> x0, starting transfers between devices: 10.3 us -> none  [the longest x3 6.23 us: extended(): lax.ppermute(lax.slice_in_dim(block, 0, width, axis=dim), axis, backward)]
  transfers between devices with their start and end apart: 9 -> 0, of which waited for: 3 -> 0; matrix products, arithmetic and copies ran while one was open for 12% -> 0% of each run, Pallas kernels for 0% -> 0%
where the time goes in v1:
time: 42.8 us; the launch traced here: 42.5 us
  Pallas kernels  36 us (84%)
  local copies, waits for them, and re-layouts  5.88 us (14%)
  between operations  0.69 us (2%)
    pallas_call x1, Pallas kernels, step(): pl.pallas_call(kernel_body, out_shape=(jax.ShapeDtypeStruct(positions.sha...  36 us
    unnamed x21, local copies, waits for them, and re-layouts  4.69 us
    pallas_call x2, local copies, waits for them, and re-layouts, step(): pl.pallas_call(kernel_body, out_shape=(jax.ShapeDtypeStruct(positions.sha...  1.19 us

profile of v1, /device:TPU:1, one launch (start us, length us, event | category | flops | bytes accessed | tf_op | source)
XLA Modules:
  0.0 42.5 jit_solution(8631948976256710631)
XLA Ops:
  0.6 0.0 copy-start
  0.6 0.7 %copy.14.pos_ref = f32[4,3,128]{2,1,0:T(4,128)S(1)} copy(f32[4,3,128]{2,0,1:T(4,128)} %param.11) | data formatting | bytes 12288 | tf_op args[0]
  1.3 0.0 copy-start.2
  1.3 0.0 copy-start.3
  1.3 0.0 copy-start.4
  1.3 0.0 copy-start.5
  1.4 0.7 %copy.15.vel_ref = f32[4,3,128]{2,1,0:T(4,128)S(1)} copy(f32[4,3,128]{2,0,1:T(4,128)} %param.12) | data formatting | bytes 12288 | tf_op args[1]
  2.1 0.0 copy-done
  2.1 0.0 copy-done.2
  2.1 0.0 copy-done.3
  2.1 0.0 copy-done.4
  2.1 0.0 copy-done.5
  2.1 0.0 copy-start.1
  2.1 0.7 %copy-done.1 = f32[2048]{0:T(1024)S(1)} copy-done((f32[2048]{0:T(1024)S(1)}, f32[2048]{0:T(1024)}, u32[]{:S(2)}) %copy-start.1) | copy-done | bytes 8216
  2.8 0.0 copy-start.6
  2.8 0.7 %copy-done.6 = f32[8]{0:T(128)S(1)} copy-done((f32[8]{0:T(128)S(1)}, f32[8]{0:T(128)}, u32[]{:S(2)}) %copy-start.6) | copy-done | bytes 56
  3.5 0.0 copy-start.7
  3.5 0.7 %copy-done.7 = f32[8]{0:T(128)S(1)} copy-done((f32[8]{0:T(128)S(1)}, f32[8]{0:T(128)}, u32[]{:S(2)}) %copy-start.7) | copy-done | bytes 56
  4.1 0.0 copy-start.8
  4.1 0.7 %copy-done.8 = f32[8]{0:T(128)S(1)} copy-done((f32[8]{0:T(128)S(1)}, f32[8]{0:T(128)}, u32[]{:S(2)}) %copy-start.8) | copy-done | bytes 56
  4.8 36.0 %pimd_step.1 = (f32[4,3,128]{2,1,0:T(4,128)S(1)}, f32[4,3,128]{2,1,0:T(4,128)S(1)}, f32[4,128]{1,0:T(4,128)S(1)}) custom-call(f32[4,3,128]{2,1,0:T(4,128)S(1)} %copy.14.pos_ref, f32[4,3,128]{2,1,0:T(4,128)S(1)} %copy.15.vel_ref, f32[4,128]{1,0:T(4,128)S(1)} %copy-done.3, s32[1,128]{1,0:T(1,128)S(1)} %bitcast.7, s32[8,128]{1,0:T(8,128)S(1)} %copy-done.2, ...), custom_call_target="tpu_custom_call" | custom-call | tf_op jit(solution)/shard_map/pimd_step/pallas_call | solution.py:521
  40.8 0.6 %copy.16 = f32[4,3,128]{2,0,1:T(4,128)} copy(f32[4,3,128]{2,1,0:T(4,128)S(1)} %get-tuple-element.3) | data formatting | bytes 12288 | tf_op jit(solution)/shard_map/pimd_step/pallas_call | solution.py:521
  41.4 0.6 %copy.17 = f32[4,3,128]{2,0,1:T(4,128)} copy(f32[4,3,128]{2,1,0:T(4,128)S(1)} %get-tuple-element.4) | data formatting | bytes 12288 | tf_op jit(solution)/shard_map/pimd_step/pallas_call | solution.py:521
  42.0 0.6 %copy.19 = f32[4,128]{1,0:T(4,128)} copy(f32[4,128]{1,0:T(4,128)S(1)} %get-tuple-element.11) | data formatting | bytes 4096
Async XLA Ops:
  0.6 1.5 %copy-start = (s32[3,2048]{1,0:T(4,128)S(1)}, s32[3,2048]{1,0:T(4,128)}, u32[]{:S(2)}) copy-start(s32[3,2048]{1,0:T(4,128)} %k_ref.1) | copy-start | bytes 73732
  1.3 0.8 %copy-start.2 = (s32[8,128]{1,0:T(8,128)S(1)}, s32[8,128]{1,0:T(8,128)}, u32[]{:S(2)}) copy-start(s32[8,128]{1,0:T(8,128)} %nbr_ref.1) | copy-start | bytes 12292
  1.3 0.8 %copy-start.3 = (f32[4,128]{1,0:T(4,128)S(1)}, f32[4,128]{1,0:T(4,128)}, u32[]{:S(2)}) copy-start(f32[4,128]{1,0:T(4,128)} %chg_ref.1) | copy-start | bytes 6148
  1.3 0.8 %copy-start.4 = (s32[128]{0:T(128)S(1)}, s32[128]{0:T(128)}, u32[]{:S(2)}) copy-start(s32[128]{0:T(128)} %param.14) | copy-start | bytes 1540
  1.3 0.8 %copy-start.5 = (f32[8]{0:T(128)S(1)}, f32[8]{0:T(128)}, u32[]{:S(2)}) copy-start(f32[8]{0:T(128)} %param.18) | copy-start | bytes 100
  2.1 0.7 %copy-start.1 = (f32[2048]{0:T(1024)S(1)}, f32[2048]{0:T(1024)}, u32[]{:S(2)}) copy-start(f32[2048]{0:T(1024)} %param.17) | copy-start | bytes 24580
  2.8 0.7 %copy-start.6 = (f32[8]{0:T(128)S(1)}, f32[8]{0:T(128)}, u32[]{:S(2)}) copy-start(f32[8]{0:T(128)} %param.19) | copy-start | bytes 100
  3.5 0.7 %copy-start.7 = (f32[8]{0:T(128)S(1)}, f32[8]{0:T(128)}, u32[]{:S(2)}) copy-start(f32[8]{0:T(128)} %param.20) | copy-start | bytes 100
  4.1 0.7 %copy-start.8 = (f32[8]{0:T(128)S(1)}, f32[8]{0:T(128)}, u32[]{:S(2)}) copy-start(f32[8]{0:T(128)} %param.21) | copy-start | bytes 100

commit v2 on v1

--- a/solution.py
+++ b/solution.py
@@ -72,20 +72,26 @@
 
 
 def kernel_body(
-    pos_ref,
-    vel_ref,
-    chg_ref,
-    spec_ref,
+    pos_hbm,
+    vel_hbm,
+    chg_hbm,
+    spec_hbm,
+    nbr_hbm,
+    k_hbm,
+    kern_hbm,
+    chi_hbm,
+    hard_hbm,
+    bond_hbm,
+    mass_hbm,
+    out_ref,
+    pos_s,
+    vel_s,
+    chg_s,
+    spec_s,
     nbr_ref,
     k_ref,
     kern_ref,
-    chi_ref,
-    hard_ref,
-    bond_ref,
-    mass_ref,
-    npos_ref,
-    nvel_ref,
-    nchg_ref,
+    tables,
     send_s,
     buf,
     nbuf,
@@ -108,6 +114,7 @@
     fsend,
     frecv,
     halo,
+    in_sem,
     s_sem,
     r_sem,
     ns_sem,
@@ -129,6 +136,27 @@
     next_bead = (bead + 1) % BEAD_AXIS
     prev_bead = (bead + BEAD_AXIS - 1) % BEAD_AXIS
 
+    loads = [
+        pltpu.make_async_copy(source, target, in_sem.at[i])
+        for i, (source, target) in enumerate(
+            (
+                (pos_hbm, pos_s),
+                (chg_hbm, chg_s),
+                (spec_hbm, spec_s),
+                (chi_hbm, tables.at[0]),
+                (hard_hbm, tables.at[1]),
+                (bond_hbm, tables.at[2]),
+                (mass_hbm, tables.at[3]),
+                (nbr_hbm, nbr_ref),
+                (k_hbm, k_ref),
+                (kern_hbm, kern_ref),
+                (vel_hbm, vel_s),
+            )
+        )
+    ]
+    for load in loads:
+        load.start()
+
     barrier = pltpu.get_barrier_semaphore()
 
     def greet(k, carry):
@@ -139,22 +167,26 @@
     for other in (next_bead, prev_bead):
         pl.semaphore_signal(barrier, inc=1, device_id={"beads": other}, device_id_type=MESH)
 
-    species = spec_ref[...]
-
-    def lookup(table):
+    for load in loads[0:7]:
+        load.wait()
+    species = spec_s[...]
+
+    def lookup(t):
         total = jnp.zeros((1, BLOCK), f32)
         for s in range(SPECIES):
-            total = jnp.where(species == s, table[0, s], total)
+            total = jnp.where(species == s, tables[t, s], total)
         return total
 
-    chi_row, hard_row, bond_row, mass_row = (lookup(t) for t in (chi_ref, hard_ref, bond_ref, mass_ref))
+    chi_row, hard_row, bond_row, mass_row = (lookup(t) for t in range(4))
     for b in range(4):
-        send_s[b, 0:3, :] = pos_ref[b]
-        send_s[b, 3:4, :] = chg_ref[b : b + 1, :]
+        for d in range(3):
+            send_s[b, d : d + 1, :] = pos_s[d, b : b + 1, :]
+        send_s[b, 3:4, :] = chg_s[b : b + 1, :]
         send_s[b, 4:5, :] = chi_row
         send_s[b, 5:6, :] = hard_row
         send_s[b, 6:7, :] = bond_row
         send_s[b, 7:8, :] = bond_row
+    loads[7].wait()
 
     pl.semaphore_wait(barrier, GROUP + 1)
 
@@ -193,14 +225,16 @@
                     pltpu.make_async_copy(source(b), store.at[slot], sem.at[slot]).start()
 
     to_next = pltpu.make_async_remote_copy(
-        pos_ref.at[3], halo.at[0], hs_sem.at[0], hr_sem.at[0], device_id={"beads": next_bead}, device_id_type=MESH
+        send_s.at[3], halo.at[0], hs_sem.at[0], hr_sem.at[0], device_id={"beads": next_bead}, device_id_type=MESH
     )
     to_prev = pltpu.make_async_remote_copy(
-        pos_ref.at[0], halo.at[1], hs_sem.at[1], hr_sem.at[1], device_id={"beads": prev_bead}, device_id_type=MESH
+        send_s.at[0], halo.at[1], hs_sem.at[1], hr_sem.at[1], device_id={"beads": prev_bead}, device_id_type=MESH
     )
     to_next.start()
     to_prev.start()
 
+    for load in loads[8:]:
+        load.wait()
     nx, ny, nz = (k_ref[d : d + 1, :] for d in range(3))
     ax, ay, az = jnp.abs(nx), jnp.abs(ny), jnp.abs(nz)
     code = jnp.where(
@@ -333,37 +367,38 @@
     def potential():
         lhs[0:ROWS, :] = expand(coef[...])
 
-        def visit(i, carry):
-            at = pl.ds(pl.multiple_of(i * 256, 256), 256)
+        for i in range(SLOTS // 2):
+            at = slice(i * 256, i * 256 + 256)
             fields = jnp.dot(lhs[0:ROWS, :], wst[:, at], preferred_element_type=f32)
             total = jnp.sum((fields * utab[:, at]).reshape(TILES, 8, 256), 0)
             row = jnp.sum(total, 0, keepdims=True)
-            phi_s[pl.ds(2 * i, 1), :] = row[:, 0:128]
-            phi_s[pl.ds(2 * i + 1, 1), :] = row[:, 128:256]
-            return carry
-
-        lax.fori_loop(0, SLOTS // 2, visit, 0)
-
-    def near_sums(own, left, right, out):
-        ext_s[0:1, :] = left
-        ext_s[1:17, :] = own
-        ext_s[17:18, :] = right
-        lane_at = lax.broadcasted_iota(jnp.int32, (8, BLOCK), 1)
-
-        def visit(j, carry):
+            phi_s[2 * i : 2 * i + 1, :] = row[:, 0:128]
+            phi_s[2 * i + 1 : 2 * i + 2, :] = row[:, 128:256]
+
+    lane_at = lax.broadcasted_iota(jnp.int32, (8, BLOCK), 1)
+
+    def near_sums(blocks, out):
+        for j in blocks:
             target = lane_at + nbuf[j]
             index = target & (BLOCK - 1)
             low, mid, high = (
                 jnp.take_along_axis(
-                    jnp.broadcast_to(ext_s[pl.ds(j + d, 1), :], (8, BLOCK)), index, axis=1, mode="promise_in_bounds"
+                    jnp.broadcast_to(ext_s[j + d : j + d + 1, :], (8, BLOCK)), index, axis=1, mode="promise_in_bounds"
                 )
                 for d in range(3)
             )
             got = jnp.where(target < 0, low, jnp.where(target >= BLOCK, high, mid))
-            out[pl.ds(j, 1), :] = jnp.sum(got, 0, keepdims=True)
-            return carry
-
-        lax.fori_loop(0, SLOTS, visit, 0)
+            out[j : j + 1, :] = jnp.sum(got, 0, keepdims=True)
+
+    def inner_near(own, out):
+        ext_s[1:17, :] = own
+        near_sums(range(1, SLOTS - 1), out)
+
+    def outer_near(own, left, right, out):
+        ext_s[0:1, :] = left
+        ext_s[1:17, :] = own
+        ext_s[17:18, :] = right
+        near_sums((0, SLOTS - 1), out)
 
     def refactor(values):
         for j in range(SLOTS):
@@ -389,10 +424,12 @@
         return carry
 
     lax.fori_loop(0, SLOTS, wait_nbr, 0)
+    inner_near(bond, nbond_s)
+    inner_near(weighted, near_s)
     exchange.wait()
     ends = ex_r[0, ROWS:EXROWS, :]
-    near_sums(bond, ends[3:4, :], ends[2:3, :], nbond_s)
-    near_sums(weighted, ends[1:2, :], ends[0:1, :], near_s)
+    outer_near(bond, ends[3:4, :], ends[2:3, :], nbond_s)
+    outer_near(weighted, ends[1:2, :], ends[0:1, :], near_s)
     mix(0, False)
     potential()
     relaxed = relax(charge, near_s[...])
@@ -400,9 +437,10 @@
     weighted = bond * relaxed
     refactor(relaxed)
     exchange = start_exchange(1, weighted)
+    inner_near(weighted, near_s)
     exchange.wait()
     ends = ex_r[1, ROWS:EXROWS, :]
-    near_sums(weighted, ends[1:2, :], ends[0:1, :], near_s)
+    outer_near(weighted, ends[1:2, :], ends[0:1, :], near_s)
     mean = mix(1, True)
     potential()
     charge = relaxed - mean
@@ -495,17 +533,17 @@
         pltpu.make_async_remote_copy(
             fsend.at[0], frecv.at[b], fs_sem.at[0], fr_sem.at[b], device_id={"atoms": partner}, device_id_type=MESH
         ).wait_recv()
-        got = frecv[b]
-        charges = got[3:4, :]
-        nchg_ref[b : b + 1, :] = charges
-        ewald_force = (-two_pi * ewald_scale) * charges * got[0:3, :]
-        here = pos_ref[b]
-        before = halo[0] if b == 0 else pos_ref[b - 1]
-        after = halo[1] if b == 3 else pos_ref[b + 1]
+    charges = frecv[:, 3, :]
+    out_ref[6] = charges
+    for d in range(3):
+        ewald_force = (-two_pi * ewald_scale) * charges * frecv[:, d, :]
+        here = pos_s[d]
+        before = jnp.concatenate([halo[0, d : d + 1, :], here[0:3, :]], 0)
+        after = jnp.concatenate([here[1:4, :], halo[1, d : d + 1, :]], 0)
         laplace = 2.0 * here - before - after
-        speed = vel_ref[b] + time_step * (ewald_force * inv_mass - spring_rate * laplace)
-        nvel_ref[b] = speed
-        npos_ref[b] = here + time_step * speed
+        speed = vel_s[d] + time_step * (ewald_force * inv_mass - spring_rate * laplace)
+        out_ref[3 + d] = speed
+        out_ref[d] = here + time_step * speed
     for m in range(4):
         home, copy = force_copy(m)
 
@@ -514,20 +552,37 @@
             copy.wait_send()
 
 
+def emit_body(packed, npos_hbm, nvel_hbm, nchg_hbm, sems):
+    copies = [
+        pltpu.make_async_copy(source, target, sems.at[i])
+        for i, (source, target) in enumerate(
+            ((packed.at[0:3], npos_hbm), (packed.at[3:6], nvel_hbm), (packed.at[6], nchg_hbm))
+        )
+    ]
+    for copy in copies:
+        copy.start()
+    for copy in copies:
+        copy.wait()
+
+
 def step(positions, velocities, charges_in, species, neighbors, k_index, kernel, chi, hard, bond, mass):
     vmem = pl.BlockSpec(memory_space=pltpu.VMEM)
-    smem = pl.BlockSpec(memory_space=pltpu.SMEM)
+    hbm = pl.BlockSpec(memory_space=pltpu.HBM)
     dma = pltpu.SemaphoreType.DMA
-    return pl.pallas_call(
+    packed = pl.pallas_call(
         kernel_body,
-        out_shape=(
-            jax.ShapeDtypeStruct(positions.shape, f32),
-            jax.ShapeDtypeStruct(velocities.shape, f32),
-            jax.ShapeDtypeStruct(charges_in.shape, f32),
-        ),
-        in_specs=[vmem] * 7 + [smem] * 4,
-        out_specs=(vmem, vmem, vmem),
+        out_shape=jax.ShapeDtypeStruct((7, 4, BLOCK), f32),
+        in_specs=[hbm] * 11,
+        out_specs=vmem,
         scratch_shapes=[
+            pltpu.VMEM((3, 4, BLOCK), f32),
+            pltpu.VMEM((3, 4, BLOCK), f32),
+            pltpu.VMEM((4, BLOCK), f32),
+            pltpu.VMEM((1, BLOCK), jnp.int32),
+            pltpu.VMEM((8, BLOCK), jnp.int32),
+            pltpu.VMEM((3, KVEC), jnp.int32),
+            pltpu.VMEM((1, KVEC), f32),
+            pltpu.SMEM((4, SPECIES), f32),
             pltpu.VMEM((4, 8, 128), f32),
             pltpu.VMEM((SLOTS, 8, 128), f32),
             pltpu.VMEM((SLOTS, 8, 128), jnp.int32),
@@ -549,7 +604,8 @@
             pltpu.VMEM((24, 128), f32),
             pltpu.VMEM((4, 8, 128), f32),
             pltpu.VMEM((4, 8, 128), f32),
-            pltpu.VMEM((2, 3, 128), f32),
+            pltpu.VMEM((2, 8, 128), f32),
+            dma((11,)),
             dma((16,)),
             dma((16,)),
             dma((16,)),
@@ -561,18 +617,31 @@
             dma((2,)),
             dma((2,)),
         ],
-        compiler_params=pltpu.CompilerParams(collective_id=0, has_side_effects=True, vmem_limit_bytes=48 * 1024 * 1024),
+        compiler_params=pltpu.CompilerParams(collective_id=0, has_side_effects=True),
         name="pimd_step",
     )(
-        positions,
-        velocities,
+        positions.transpose(1, 0, 2),
+        velocities.transpose(1, 0, 2),
         charges_in,
         species.reshape(1, BLOCK),
         neighbors,
         k_index,
         kernel.reshape(1, KVEC),
-        *(t.reshape(1, SPECIES) for t in (chi, hard, bond, mass)),
+        chi,
+        hard,
+        bond,
+        mass,
     )
+    spatial = jax.ShapeDtypeStruct((3, 4, BLOCK), f32)
+    new_positions, new_velocities, charges = pl.pallas_call(
+        emit_body,
+        out_shape=(spatial, spatial, jax.ShapeDtypeStruct((4, BLOCK), f32)),
+        in_specs=[vmem],
+        out_specs=(hbm, hbm, hbm),
+        scratch_shapes=[dma((3,))],
+        name="emit",
+    )(packed)
+    return new_positions.transpose(1, 0, 2), new_velocities.transpose(1, 0, 2), charges
 
 
 def solution(mesh):

time: 42.8 us -> 33.3 us (0.78)
  local copies, waits for them, and re-layouts: 5.88 us -> 0 us
  Pallas kernels: 36 us -> 32.4 us
    unnamed x21 -> x0, local copies, waits for them, and re-layouts: 4.69 us -> none
    pallas_call x1 -> x2, Pallas kernels: 36 us -> 32.4 us  [the longest x1 31.1 us: step(): pl.pallas_call(kernel_body, out_shape=jax.ShapeDtypeStruct((7, 4, BLOCK),...]
    pallas_call x2 -> x0, local copies, waits for them, and re-layouts: 1.19 us -> none  [step(): pl.pallas_call(kernel_body, out_shape=(jax.ShapeDtypeStruct(positions.sha...]
where the time goes in v2:
time: 33.3 us; the launch traced here: 33.1 us
  Pallas kernels  32.4 us (97%)
  between operations  0.64 us (2%)
    pallas_call x1, Pallas kernels, step(): pl.pallas_call(kernel_body, out_shape=jax.ShapeDtypeStruct((7, 4, BLOCK),...  31.1 us
    pallas_call x1, Pallas kernels, step(): pl.pallas_call(emit_body, out_shape=(spatial, spatial, jax.ShapeDtypeStru...  1.34 us

profile of v2, /device:TPU:1, one launch (start us, length us, event | category | flops | bytes accessed | tf_op | source)
XLA Modules:
  0.0 33.1 jit_solution(3052967303777604218)
XLA Ops:
  0.6 31.1 %pimd_step.1.packed = f32[7,4,128]{2,1,0:T(4,128)} custom-call(f32[3,4,128]{2,1,0:T(4,128)} %bitcast.7, f32[3,4,128]{2,1,0:T(4,128)} %bitcast.8, f32[4,128]{1,0:T(4,128)} %chg_hbm.1, s32[1,128]{1,0:T(1,128)} %bitcast.9, s32[8,128]{1,0:T(8,128)} %nbr_hbm.1, s32[3,2048]{1,0:T(4,128)} %k_hbm.1, f32[1,2048]{1,0:T(1,128)} %bitcast.6, f32[8]{0:T(128)} %chi_hbm.1, ...), custom_call_target="tpu_custom_call" | custom-call | tf_op jit(solution)/shard_map/pimd_step/pallas_call | solution.py:572
  31.7 1.3 %emit.1 = (f32[3,4,128]{2,1,0:T(4,128)}, f32[3,4,128]{2,1,0:T(4,128)}, f32[4,128]{1,0:T(4,128)}) custom-call(f32[7,4,128]{2,1,0:T(4,128)} %pimd_step.1.packed), custom_call_target="tpu_custom_call" | custom-call | tf_op jit(solution)/shard_map/emit/pallas_call | solution.py:636

commit v3 on v2

--- a/solution.py
+++ b/solution.py
@@ -10,7 +10,6 @@
 KVEC = 2048
 SPECIES = 8
 ATOMS = 4096
-GROUP = 32
 BEAD_AXIS = 8
 BLOCK = 128
 SLOTS = 16
@@ -18,6 +17,8 @@
 TILES = 38
 ROWS = TILES * 8
 EXROWS = ROWS + 8
+REST = 6
+PARTS = ((0, REST + 12, (0, 1, 2)), (REST + 12, TILES, (3, 4, 5, 6, 7)))
 
 two_pi = 2.0 * math.pi
 ewald_scale = 4.0 / math.sqrt(KVEC * ATOMS)
@@ -58,17 +59,17 @@
 
 
 def flip(x):
-    lane = lax.broadcasted_iota(jnp.int32, x.shape, 1)
-    return jnp.where(lane < 16, pltpu.roll(x, 112, 1), pltpu.roll(x, 16, 1))
+    return pltpu.roll(x, 16, 1)
 
 
 def core_tile(ta, tb, a):
-    return 16 * ta + 8 * tb + a
+    return REST + 4 * a + 2 * ta + tb
 
 
 def expand(coeff):
     high, low = split(coeff)
-    return (high.astype(f32) + pltpu.roll(low, 32, 1) + pltpu.roll(high.astype(f32), 64, 1)).astype(bf16)
+    group = lax.broadcasted_iota(jnp.int32, coeff.shape, 1) // 32
+    return jnp.where(group == 1, low, high.astype(f32)).astype(bf16)
 
 
 def kernel_body(
@@ -96,16 +97,15 @@
     buf,
     nbuf,
     utab,
-    uhi,
-    ulo,
+    ubf,
     wtab,
     wst,
     acols,
     etab,
     ex_s,
     ex_r,
-    factor,
-    coef,
+    acc,
+    gtab,
     lhs,
     phi_s,
     near_s,
@@ -159,11 +159,22 @@
 
     barrier = pltpu.get_barrier_semaphore()
 
-    def greet(k, carry):
-        pl.semaphore_signal(barrier, inc=1, device_id={"atoms": (me + k) % GROUP}, device_id_type=MESH)
-        return carry
-
-    lax.fori_loop(1, GROUP, greet, 0)
+    def greet(x, zz, c):
+        pl.semaphore_signal(barrier, inc=1, device_id={"atoms": 16 * x + 2 * zz + c}, device_id_type=MESH)
+
+    odd = x_lo ^ core
+    for o in (4, 3, 5, 2, 6, 1, 7, 0):
+        zz = (z + o) % 8
+        greet(1 - x_lo, zz, core)
+        greet(x_lo, zz, 1 - core)
+        if o:
+            greet(x_lo ^ odd, zz, core ^ odd)
+        else:
+
+            @pl.when(odd == 1)
+            def _():
+                greet(x_lo ^ odd, zz, core ^ odd)
+
     for other in (next_bead, prev_bead):
         pl.semaphore_signal(barrier, inc=1, device_id={"beads": other}, device_id_type=MESH)
 
@@ -188,7 +199,7 @@
         send_s[b, 7:8, :] = bond_row
     loads[7].wait()
 
-    pl.semaphore_wait(barrier, GROUP + 1)
+    pl.semaphore_wait(barrier, 25 + odd)
 
     slot = z * 2 + core
 
@@ -260,10 +271,27 @@
         grid = term if grid is None else grid + term
     lane = lax.broadcasted_iota(jnp.int32, (96, 128), 1)
     for j in range(4):
-        moved = grid if j == 0 else pltpu.roll(grid, 128 - 32 * j, 1)
-        etab[j] = jnp.where(lane < 32, moved, 0.0)
-
-    factor[...] = jnp.zeros((ROWS, 128), f32)
+        kept = jnp.where(lane // 32 == j, grid, 0.0)
+        kept = kept + pltpu.roll(kept, 64, 1)
+        etab[j] = kept + pltpu.roll(kept, 32, 1)
+
+    ex_s[0, 8:EXROWS, :] = jnp.zeros((ROWS, 128), f32)
+    ex_s[3, 8:EXROWS, :] = jnp.zeros((ROWS, 128), f32)
+    ex_s[3, 0:8, :] = jnp.zeros((8, 128), f32)
+
+    def ubf_rows(part):
+        low, high, _ = PARTS[part]
+        return slice(16 * low, 16 * high)
+
+    def fold(part, product):
+        half = 8 * (PARTS[part][1] - PARTS[part][0])
+        return product[0:half, :] + product[half:, :]
+
+    def accumulate(part, rows, at, columns):
+        product = fold(part, lax.dot_general(ubf[rows, at], columns, NT, preferred_element_type=f32))
+        low, high, _ = PARTS[part]
+        ex_s[0, 8 + 8 * low : 8 + 8 * high, :] += product[:, 0:128]
+        ex_s[3, 8 + 8 * low : 8 + 8 * high, :] += product[:, 128:256]
     first = jnp.where(lax.broadcasted_iota(jnp.int32, (8, 512), 0) == 0, 1.0, 0.0)
     zero8 = jnp.zeros((8, 512), f32)
 
@@ -287,16 +315,18 @@
             both = jnp.concatenate([low_tile, high_tile], 0)
             utab[8 * t : 8 * t + 16, at] = both
             high, low = split(both)
-            uhi[8 * t : 8 * t + 16, at] = high
-            ulo[8 * t : 8 * t + 16, at] = low.astype(bf16)
-
-        for ta, u in ((0, cu), (1, su)):
-            for tb, v in ((0, cv), (1, sv)):
-                for a in range(0, 8, 2):
-                    put(core_tile(ta, tb, a), u[a : a + 1, :] * v, u[a + 1 : a + 2, :] * v)
-        put(32, cv, sv)
-        put(34, cu, su)
-        put(36, first, zero8)
+            first_row = 8 * (t + (0 if t < PARTS[1][0] else PARTS[1][0]))
+            ubf[first_row : first_row + 16, at] = high
+            first_row += 8 * (PARTS[0][1] if t < PARTS[1][0] else TILES - PARTS[1][0])
+            ubf[first_row : first_row + 16, at] = low.astype(bf16)
+
+        put(0, first, zero8)
+        put(2, cv, sv)
+        put(4, cu, su)
+        for a in range(8):
+            for ta, u in ((0, cu), (1, su)):
+                here = u[a : a + 1, :]
+                put(core_tile(ta, 0, a), here * cv, here * sv)
 
         w = jnp.concatenate([cw, first, sw, zero8], 0)
         wtab[:, at] = w
@@ -307,11 +337,9 @@
         wst[64:96, at] = wlo
         wst[96:128, at] = jnp.zeros((32, 512), bf16)
         qhi, qlo = split(w * rows[3])
-        a_block = jnp.concatenate([qhi, qlo.astype(bf16), whi, wlo], 0)
-        acols[:, at] = a_block
-        factor[...] += lax.dot_general(uhi[:, at], a_block, NT, preferred_element_type=f32) + lax.dot_general(
-            ulo[:, at], a_block, NT, preferred_element_type=f32
-        )
+        qlo = qlo.astype(bf16)
+        for part in range(2):
+            accumulate(part, ubf_rows(part), at, jnp.concatenate([qhi, qlo, qhi, qlo, whi, wlo, whi, wlo], 0))
         return carry
 
     lax.fori_loop(0, 4, arrive, 0)
@@ -321,59 +349,91 @@
     inv_hard = 1.0 / buf[:, 5, :]
     bond = buf[:, 6, :]
 
-    def start_exchange(r, weighted):
-        ex_s[r, 0:ROWS, :] = factor[...]
-        ends = jnp.concatenate(
+    def share(r, part):
+        low, high, _ = PARTS[part]
+        rows = pl.ds(0, 8 + 8 * high) if part == 0 else pl.ds(8 + 8 * low, 8 * (high - low))
+        return pltpu.make_async_remote_copy(
+            ex_s.at[r, rows],
+            ex_r.at[r, rows],
+            xs_sem.at[r, part],
+            xr_sem.at[r, part],
+            device_id={"atoms": partner},
+            device_id_type=MESH,
+        )
+
+    def put_ends(r, weighted):
+        ex_s[r, 0:8, :] = jnp.concatenate(
             [weighted[0:1, :], weighted[15:16, :], bond[0:1, :], bond[15:16, :], jnp.zeros((4, 128), f32)], 0
         )
-        ex_s[r, ROWS:EXROWS, :] = ends
-        copy = pltpu.make_async_remote_copy(
-            ex_s.at[r], ex_r.at[r], xs_sem.at[r], xr_sem.at[r], device_id={"atoms": partner}, device_id_type=MESH
-        )
-        copy.start()
-        return copy
-
-    def mix(r, centre):
-        total = ex_s[r, 0:ROWS, :] + ex_r[r, 0:ROWS, :]
-        total = total + pltpu.roll(total, 96, 1)
-        mean = 0.0
-        if centre:
-            mean = total[8 * 36 : 8 * 36 + 1, 8:9] * (1.0 / ATOMS)
-            total = total - mean * pltpu.roll(total, 64, 1)
-        for ta in range(2):
-            for tb in range(2):
-                for a in range(8):
-                    here = tile(total, core_tile(ta, tb, a))
-                    both = tile(total, core_tile(1 - ta, 1 - tb, a))
-                    over_b = flip(tile(total, core_tile(ta, 1 - tb, a)))
-                    over_a = flip(tile(total, core_tile(1 - ta, tb, a)))
-                    e = [etab[j, 8 * a : 8 * a + 8, :] for j in range(4)]
-                    out = e[0] * here
+
+    ones_share = pltpu.make_async_remote_copy(
+        ex_s.at[3], ex_r.at[3], xs_sem.at[3, 0], xr_sem.at[3, 0], device_id={"atoms": partner}, device_id_type=MESH
+    )
+
+    lane16 = lax.broadcasted_iota(jnp.int32, (16, 128), 1)
+    number = jnp.where((lane16 & 15) < 8, (lane16 & 15) + 1, 0).astype(f32)
+    slope = jnp.where((lane16 & 16) == 0, number, -number)
+
+    def mix(r, part, mean, slopes):
+        low, high, numbers = PARTS[part]
+        rows = slice(8 + 8 * low, 8 + 8 * high)
+        total = ex_s[r, rows, :] + ex_r[r, rows, :]
+        total = total + pltpu.roll(total, 32, 1)
+        if r > 0:
+            if part == 0:
+                mean = total[0:1, 8:9] * (1.0 / ATOMS)
+            total = total - mean * gtab[8 * low : 8 * high, :]
+        swapped = flip(total)
+
+        def store(t, pair):
+            lhs[8 * t : 8 * t + 16, :] = expand(pair)
+            if slopes:
+                lhs[ROWS + 8 * t : ROWS + 8 * t + 16, :] = expand(flip(pair) * slope)
+
+        if part == 0:
+            zero = jnp.zeros((8, 128), f32)
+            store(0, jnp.concatenate([etab[0, 80:88, :] * tile(total, 0), zero], 0))
+            for t, row, j in ((2, 64, 1), (4, 72, 2)):
+                e0 = etab[0, row : row + 8, :]
+                ej = etab[j, row : row + 8, :]
+                pair = [
+                    e0 * tile(total, t) + ej * tile(swapped, t + 1),
+                    e0 * tile(total, t + 1) - ej * tile(swapped, t),
+                ]
+                store(t, jnp.concatenate(pair, 0))
+        for a in numbers:
+            e = [etab[j, 8 * a : 8 * a + 8, :] for j in range(4)]
+            for ta in range(2):
+                pair = []
+                for tb in range(2):
+                    both = tile(total, core_tile(1 - ta, 1 - tb, a) - low)
+                    over_b = tile(swapped, core_tile(ta, 1 - tb, a) - low)
+                    over_a = tile(swapped, core_tile(1 - ta, tb, a) - low)
+                    out = e[0] * tile(total, core_tile(ta, tb, a) - low)
                     out = out + e[3] * both if ta == tb else out - e[3] * both
                     out = out + e[1] * over_b if tb == 0 else out - e[1] * over_b
                     out = out + e[2] * over_a if ta == 0 else out - e[2] * over_a
-                    t = core_tile(ta, tb, a)
-                    coef[8 * t : 8 * t + 8, :] = out
-        for first_tile, row, j in ((32, 64, 1), (34, 72, 2)):
-            e0 = etab[0, row : row + 8, :]
-            ej = etab[j, row : row + 8, :]
-            c, s = tile(total, first_tile), tile(total, first_tile + 1)
-            coef[8 * first_tile : 8 * first_tile + 8, :] = e0 * c + ej * flip(s)
-            coef[8 * first_tile + 8 : 8 * first_tile + 16, :] = e0 * s - ej * flip(c)
-        coef[8 * 36 : 8 * 37, :] = etab[0, 80:88, :] * tile(total, 36)
-        coef[8 * 37 : 8 * 38, :] = jnp.zeros((8, 128), f32)
+                    pair.append(out)
+                store(core_tile(ta, 0, a), jnp.concatenate(pair, 0))
         return mean
 
-    def potential():
-        lhs[0:ROWS, :] = expand(coef[...])
-
+    def potential(part):
+        low, high, _ = PARTS[part]
+        rows = slice(8 * low, 8 * high)
         for i in range(SLOTS // 2):
             at = slice(i * 256, i * 256 + 256)
-            fields = jnp.dot(lhs[0:ROWS, :], wst[:, at], preferred_element_type=f32)
-            total = jnp.sum((fields * utab[:, at]).reshape(TILES, 8, 256), 0)
-            row = jnp.sum(total, 0, keepdims=True)
-            phi_s[2 * i : 2 * i + 1, :] = row[:, 0:128]
-            phi_s[2 * i + 1 : 2 * i + 2, :] = row[:, 128:256]
+            fields = jnp.dot(lhs[rows, :], wst[:, at], preferred_element_type=f32)
+            sums = [None] * 4
+            for t in range(low, high):
+                term = tile(fields, t - low) * utab[8 * t : 8 * t + 8, at]
+                sums[t % 4] = term if sums[t % 4] is None else sums[t % 4] + term
+            total = (sums[0] + sums[1]) + (sums[2] + sums[3])
+            if part == 0:
+                acc[0, :, at] = total
+            else:
+                row = jnp.sum(total + acc[0, :, at], 0, keepdims=True)
+                phi_s[2 * i : 2 * i + 1, :] = row[:, 0:128]
+                phi_s[2 * i + 1 : 2 * i + 2, :] = row[:, 128:256]
 
     lane_at = lax.broadcasted_iota(jnp.int32, (8, BLOCK), 1)
 
@@ -400,22 +460,34 @@
         ext_s[17:18, :] = right
         near_sums((0, SLOTS - 1), out)
 
-    def refactor(values):
-        for j in range(SLOTS):
-            at = slice(j * BLOCK, (j + 1) * BLOCK)
-            qhi, qlo = split(wtab[:, at] * values[j : j + 1, :])
-            acols[0:32, at] = qhi
-            acols[32:64, at] = qlo.astype(bf16)
-        factor[...] = lax.dot_general(uhi[...], acols[...], NT, preferred_element_type=f32) + lax.dot_general(
-            ulo[...], acols[...], NT, preferred_element_type=f32
+    def refactor(r, values):
+        total = None
+        rows = ubf_rows(0)
+        for k in range(4):
+            for j in range(4 * k, 4 * k + 4):
+                at = slice(j * BLOCK, (j + 1) * BLOCK)
+                qhi, qlo = split(wtab[:, at] * values[j : j + 1, :])
+                qlo = qlo.astype(bf16)
+                acols[:, at] = jnp.concatenate([qhi, qlo, qhi, qlo], 0)
+            at = slice(512 * k, 512 * k + 512)
+            term = lax.dot_general(ubf[rows, at], acols[:, at], NT, preferred_element_type=f32)
+            total = term if total is None else total + term
+        ex_s[r, 8 : 8 + 8 * PARTS[0][1], :] = fold(0, total)
+        share(r, 0).start()
+        ex_s[r, 8 + 8 * PARTS[1][0] : EXROWS, :] = fold(
+            1, lax.dot_general(ubf[ubf_rows(1), :], acols[...], NT, preferred_element_type=f32)
         )
+        share(r, 1).start()
 
     def relax(charge, near):
         potential_here = ewald_scale * phi_s[...]
         return 0.5 * charge + 0.5 * (-(chi + potential_here + bond * near) * inv_hard)
 
     weighted = bond * charge
-    exchange = start_exchange(0, weighted)
+    put_ends(0, weighted)
+    share(0, 0).start()
+    share(0, 1).start()
+    ones_share.start()
 
     def wait_nbr(j, carry):
         pltpu.make_async_remote_copy(
@@ -426,75 +498,88 @@
     lax.fori_loop(0, SLOTS, wait_nbr, 0)
     inner_near(bond, nbond_s)
     inner_near(weighted, near_s)
-    exchange.wait()
-    ends = ex_r[0, ROWS:EXROWS, :]
+    share(0, 0).wait()
+    mix(0, 0, None, False)
+    potential(0)
+    ends = ex_r[0, 0:8, :]
     outer_near(bond, ends[3:4, :], ends[2:3, :], nbond_s)
     outer_near(weighted, ends[1:2, :], ends[0:1, :], near_s)
-    mix(0, False)
-    potential()
+    share(0, 1).wait()
+    mix(0, 1, None, False)
+    potential(1)
     relaxed = relax(charge, near_s[...])
+    ones_share.wait()
+    weight_of_ones = ex_s[3, 8:EXROWS, :] + ex_r[3, 8:EXROWS, :]
+    gtab[...] = weight_of_ones + pltpu.roll(weight_of_ones, 32, 1)
 
     weighted = bond * relaxed
-    refactor(relaxed)
-    exchange = start_exchange(1, weighted)
+    put_ends(1, weighted)
+    refactor(1, relaxed)
     inner_near(weighted, near_s)
-    exchange.wait()
-    ends = ex_r[1, ROWS:EXROWS, :]
+    share(1, 0).wait()
+    mean = mix(1, 0, None, False)
+    potential(0)
+    ends = ex_r[1, 0:8, :]
     outer_near(weighted, ends[1:2, :], ends[0:1, :], near_s)
-    mean = mix(1, True)
-    potential()
+    share(1, 1).wait()
+    mix(1, 1, mean, False)
+    potential(1)
     charge = relaxed - mean
     relaxed = relax(charge, near_s[...] - mean * nbond_s[...])
 
-    refactor(relaxed)
-    exchange = start_exchange(2, bond * relaxed)
-    exchange.wait()
-    mean = mix(2, True)
+    put_ends(2, relaxed)
+    refactor(2, relaxed)
+
+    ones = lax.broadcasted_iota(jnp.int32, (8, 256), 0).astype(f32) + 1.0
+
+    def force(part):
+        low, high, numbers = PARTS[part]
+        for i in range(2):
+            at = pl.ds(pl.multiple_of(quad * 512 + i * 256, 256), 256)
+            keep = slice(i * 256, i * 256 + 256)
+            plain = jnp.dot(lhs[8 * low : 8 * high, :], wst[:, at], preferred_element_type=f32)
+            sloped = jnp.dot(lhs[ROWS + 8 * low : ROWS + 8 * high, :], wst[:, at], preferred_element_type=f32)
+            basis = {t: utab[8 * t : 8 * t + 8, at] for t in range(low, high)}
+            f = {t: tile(plain, t - low) for t in range(low, high)}
+            dz = [None] * 4
+            for t in range(low, high):
+                term = basis[t] * tile(sloped, t - low)
+                dz[t % 4] = term if dz[t % 4] is None else dz[t % 4] + term
+            dz = (dz[0] + dz[1]) + (dz[2] + dz[3])
+
+            def turn(c, s):
+                return basis[c] * f[s] - basis[s] * f[c]
+
+            dx = dy = None
+            for a in numbers:
+                along_x = turn(core_tile(0, 0, a), core_tile(1, 0, a)) + turn(core_tile(0, 1, a), core_tile(1, 1, a))
+                along_y = turn(core_tile(0, 0, a), core_tile(0, 1, a)) + turn(core_tile(1, 0, a), core_tile(1, 1, a))
+                along_x = (a + 1.0) * along_x
+                dx = along_x if dx is None else dx + along_x
+                dy = along_y if dy is None else dy + along_y
+            if part == 0:
+                acc[0, :, keep] = dx + ones * turn(4, 5)
+                acc[1, :, keep] = ones * (dy + turn(2, 3))
+                acc[2, :, keep] = dz
+            else:
+                dx = dx + acc[0, :, keep]
+                dy = ones * dy + acc[1, :, keep]
+                dz = dz + acc[2, :, keep]
+                dx, dy, dz = (jnp.sum(d, 0, keepdims=True) for d in (dx, dy, dz))
+                for m in range(2):
+                    own = near_s[pl.ds(quad * 4 + 2 * i + m, 1), :]
+                    piece = slice(128 * m, 128 * m + 128)
+                    fsend[2 * i + m] = jnp.concatenate(
+                        [dx[:, piece], dy[:, piece], dz[:, piece], own, jnp.zeros((4, 128), f32)], 0
+                    )
+
+    share(2, 0).wait()
+    mean = mix(2, 0, None, True)
     near_s[...] = relaxed - mean
-
-    lane = lax.broadcasted_iota(jnp.int32, (ROWS, 128), 1)
-    number = jnp.where((lane & 15) < 8, (lane & 15) + 1, 0).astype(f32)
-    slope = jnp.where(lane < 16, number, -number)
-    whole = coef[...]
-    lhs[0:ROWS, :] = expand(whole)
-    lhs[ROWS : 2 * ROWS, :] = expand(jnp.where(lane < 32, flip(whole) * slope, 0.0))
-    ones = lax.broadcasted_iota(jnp.int32, (8, 256), 0).astype(f32) + 1.0
-
-    def force(i, carry):
-        at = pl.ds(pl.multiple_of(quad * 512 + i * 256, 256), 256)
-        fields = jnp.dot(lhs[...], wst[:, at], preferred_element_type=f32)
-        basis = [utab[8 * t : 8 * t + 8, at] for t in range(37)]
-
-        def plain(t):
-            return fields[8 * t : 8 * t + 8, :]
-
-        dz = basis[0] * fields[ROWS : ROWS + 8, :]
-        for t in range(1, 37):
-            dz = dz + basis[t] * fields[ROWS + 8 * t : ROWS + 8 * t + 8, :]
-        dx = jnp.zeros((8, 256), f32)
-        for a in range(8):
-            term = jnp.zeros((8, 256), f32)
-            for tb in range(2):
-                c, s = core_tile(0, tb, a), core_tile(1, tb, a)
-                term = term + basis[c] * plain(s) - basis[s] * plain(c)
-            dx = dx + (a + 1.0) * term
-        dx = dx + ones * (basis[34] * plain(35) - basis[35] * plain(34))
-        dy = basis[32] * plain(33) - basis[33] * plain(32)
-        for ta in range(2):
-            for a in range(8):
-                c, s = core_tile(ta, 0, a), core_tile(ta, 1, a)
-                dy = dy + basis[c] * plain(s) - basis[s] * plain(c)
-        dy = dy * ones
-        dx, dy, dz = (jnp.sum(d, 0, keepdims=True) for d in (dx, dy, dz))
-        for m in range(2):
-            own = near_s[pl.ds(quad * 4 + 2 * i + m, 1), :]
-            piece = slice(128 * m, 128 * m + 128)
-            fsend[2 * i + m] = jnp.concatenate(
-                [dx[:, piece], dy[:, piece], dz[:, piece], own, jnp.zeros((4, 128), f32)], 0
-            )
-        return carry
-
-    lax.fori_loop(0, 2, force, 0)
+    force(0)
+    share(2, 1).wait()
+    mix(2, 1, mean, True)
+    force(1)
 
     my_bead = 2 * x_lo + z % 2
 
@@ -571,7 +656,7 @@
     dma = pltpu.SemaphoreType.DMA
     packed = pl.pallas_call(
         kernel_body,
-        out_shape=jax.ShapeDtypeStruct((7, 4, BLOCK), f32),
+        out_shape=pltpu.VMEM((7, 4, BLOCK), f32),
         in_specs=[hbm] * 11,
         out_specs=vmem,
         scratch_shapes=[
@@ -587,15 +672,14 @@
             pltpu.VMEM((SLOTS, 8, 128), f32),
             pltpu.VMEM((SLOTS, 8, 128), jnp.int32),
             pltpu.VMEM((ROWS, HALF), f32),
-            pltpu.VMEM((ROWS, HALF), bf16),
-            pltpu.VMEM((ROWS, HALF), bf16),
+            pltpu.VMEM((2 * ROWS, HALF), bf16),
             pltpu.VMEM((32, HALF), f32),
             pltpu.VMEM((128, HALF), bf16),
             pltpu.VMEM((128, HALF), bf16),
             pltpu.VMEM((4, 96, 128), f32),
-            pltpu.VMEM((3, EXROWS, 128), f32),
-            pltpu.VMEM((3, EXROWS, 128), f32),
-            pltpu.VMEM((ROWS, 128), f32),
+            pltpu.VMEM((4, EXROWS, 128), f32),
+            pltpu.VMEM((4, EXROWS, 128), f32),
+            pltpu.VMEM((3, 8, HALF), f32),
             pltpu.VMEM((ROWS, 128), f32),
             pltpu.VMEM((2 * ROWS, 128), bf16),
             pltpu.VMEM((SLOTS, 128), f32),
@@ -610,8 +694,8 @@
             dma((16,)),
             dma((16,)),
             dma((16,)),
-            dma((3,)),
-            dma((3,)),
+            dma((4, 2)),
+            dma((4, 2)),
             dma((4,)),
             dma((4,)),
             dma((2,)),
@@ -640,7 +724,7 @@
         out_specs=(hbm, hbm, hbm),
         scratch_shapes=[dma((3,))],
         name="emit",
-    )(packed)
+    )(pltpu.with_memory_space_constraint(packed, pltpu.VMEM))
     return new_positions.transpose(1, 0, 2), new_velocities.transpose(1, 0, 2), charges
 
 

time: 33.3 us -> 30.4 us (0.913)
  Pallas kernels: 32.4 us -> 29.6 us
    pallas_call x1, Pallas kernels: 31.1 us -> 29 us  [step(): pl.pallas_call(kernel_body, out_shape=pltpu.VMEM((7, 4, BLOCK), f32), in_...]
    pallas_call x1, Pallas kernels: 1.34 us -> 0.63 us  [step(): pl.pallas_call(emit_body, out_shape=(spatial, spatial, jax.ShapeDtypeStru...]
where the time goes in v3:
time: 30.4 us; the launch traced here: 30.2 us
  Pallas kernels  29.6 us (97%)
  between operations  0.64 us (2%)
    pallas_call x1, Pallas kernels, step(): pl.pallas_call(kernel_body, out_shape=pltpu.VMEM((7, 4, BLOCK), f32), in_...  29 us
    pallas_call x1, Pallas kernels, step(): pl.pallas_call(emit_body, out_shape=(spatial, spatial, jax.ShapeDtypeStru...  0.63 us

profile of v3, /device:TPU:1, one launch (start us, length us, event | category | flops | bytes accessed | tf_op | source)
XLA Modules:
  0.0 30.2 jit_solution(4140119471161389230)
XLA Ops:
  0.6 29.0 %pimd_step.1.packed = f32[7,4,128]{2,1,0:T(4,128)S(1)} custom-call(f32[3,4,128]{2,1,0:T(4,128)} %bitcast.7, f32[3,4,128]{2,1,0:T(4,128)} %bitcast.8, f32[4,128]{1,0:T(4,128)} %chg_hbm.1, s32[1,128]{1,0:T(1,128)} %bitcast.9, s32[8,128]{1,0:T(8,128)} %nbr_hbm.1, s32[3,2048]{1,0:T(4,128)} %k_hbm.1, f32[1,2048]{1,0:T(1,128)} %bitcast.6, f32[8]{0:T(128)} %chi_hbm.1, ...), custom_call_target="tpu_custom_call" | custom-call | tf_op jit(solution)/shard_map/pimd_step/pallas_call | solution.py:657
  29.6 0.6 %emit.1 = (f32[3,4,128]{2,1,0:T(4,128)}, f32[3,4,128]{2,1,0:T(4,128)}, f32[4,128]{1,0:T(4,128)}) custom-call(f32[7,4,128]{2,1,0:T(4,128)S(1)} %pimd_step.1.packed), custom_call_target="tpu_custom_call" | custom-call | tf_op jit(solution)/shard_map/emit/pallas_call | solution.py:720

commit v4 on v3

--- a/solution.py
+++ b/solution.py
@@ -16,9 +16,11 @@
 HALF = SLOTS * BLOCK
 TILES = 38
 ROWS = TILES * 8
-EXROWS = ROWS + 8
+GROWS = 176
+EXROWS = GROWS + 8
 REST = 6
 PARTS = ((0, REST + 12, (0, 1, 2)), (REST + 12, TILES, (3, 4, 5, 6, 7)))
+GPARTS = ((0, REST + 4), (REST + 4, GROWS // 8))
 
 two_pi = 2.0 * math.pi
 ewald_scale = 4.0 / math.sqrt(KVEC * ATOMS)
@@ -97,10 +99,10 @@
     buf,
     nbuf,
     utab,
-    ubf,
-    wtab,
+    gbf,
+    gone,
+    wcol,
     wst,
-    acols,
     etab,
     ex_s,
     ex_r,
@@ -136,6 +138,27 @@
     next_bead = (bead + 1) % BEAD_AXIS
     prev_bead = (bead + BEAD_AXIS - 1) % BEAD_AXIS
 
+    barrier = pltpu.get_barrier_semaphore()
+
+    def greet(x, zz, c):
+        pl.semaphore_signal(barrier, inc=1, device_id={"atoms": 16 * x + 2 * zz + c}, device_id_type=MESH)
+
+    odd = x_lo ^ core
+    for o in (4, 3, 5, 2, 6, 1, 7, 0):
+        zz = (z + o) % 8
+        greet(1 - x_lo, zz, core)
+        greet(x_lo, zz, 1 - core)
+        if o:
+            greet(x_lo ^ odd, zz, core ^ odd)
+        else:
+
+            @pl.when(odd == 1)
+            def _():
+                greet(x_lo ^ odd, zz, core ^ odd)
+
+    for other in (next_bead, prev_bead):
+        pl.semaphore_signal(barrier, inc=1, device_id={"beads": other}, device_id_type=MESH)
+
     loads = [
         pltpu.make_async_copy(source, target, in_sem.at[i])
         for i, (source, target) in enumerate(
@@ -156,27 +179,6 @@
     ]
     for load in loads:
         load.start()
-
-    barrier = pltpu.get_barrier_semaphore()
-
-    def greet(x, zz, c):
-        pl.semaphore_signal(barrier, inc=1, device_id={"atoms": 16 * x + 2 * zz + c}, device_id_type=MESH)
-
-    odd = x_lo ^ core
-    for o in (4, 3, 5, 2, 6, 1, 7, 0):
-        zz = (z + o) % 8
-        greet(1 - x_lo, zz, core)
-        greet(x_lo, zz, 1 - core)
-        if o:
-            greet(x_lo ^ odd, zz, core ^ odd)
-        else:
-
-            @pl.when(odd == 1)
-            def _():
-                greet(x_lo ^ odd, zz, core ^ odd)
-
-    for other in (next_bead, prev_bead):
-        pl.semaphore_signal(barrier, inc=1, device_id={"beads": other}, device_id_type=MESH)
 
     for load in loads[0:7]:
         load.wait()
@@ -275,23 +277,38 @@
         kept = kept + pltpu.roll(kept, 64, 1)
         etab[j] = kept + pltpu.roll(kept, 32, 1)
 
-    ex_s[0, 8:EXROWS, :] = jnp.zeros((ROWS, 128), f32)
-    ex_s[3, 8:EXROWS, :] = jnp.zeros((ROWS, 128), f32)
-    ex_s[3, 0:8, :] = jnp.zeros((8, 128), f32)
-
-    def ubf_rows(part):
-        low, high, _ = PARTS[part]
+    ex_s[0] = jnp.zeros((EXROWS, 256), f32)
+    ex_s[3] = jnp.zeros((EXROWS, 256), f32)
+    ex_s[1, 0:8, :] = jnp.zeros((8, 256), f32)
+    ex_s[2, 0:8, :] = jnp.zeros((8, 256), f32)
+
+    def gbf_rows(part):
+        low, high = GPARTS[part]
         return slice(16 * low, 16 * high)
 
-    def fold(part, product):
-        half = 8 * (PARTS[part][1] - PARTS[part][0])
+    def ex_rows(part):
+        low, high = GPARTS[part]
+        return slice(8 + 8 * low, 8 + 8 * high)
+
+    def columns(values):
+        high, low = split(values)
+        high = high.astype(f32)
+        pieces = [high[0:64], low[0:64], high[64:96], low[64:96], high[64:96], low[64:96]]
+        return jnp.concatenate(pieces, 0)
+
+    def put_split(target, g, at, both):
+        part = 0 if g < GPARTS[0][1] else 1
+        low, high = GPARTS[part]
+        row = 8 * (g + low)
+        ghigh, glow = split(both)
+        target[row : row + 16, at] = ghigh
+        row += 8 * (high - low)
+        target[row : row + 16, at] = glow.astype(bf16)
+
+    def fold(product):
+        half = product.shape[0] // 2
         return product[0:half, :] + product[half:, :]
 
-    def accumulate(part, rows, at, columns):
-        product = fold(part, lax.dot_general(ubf[rows, at], columns, NT, preferred_element_type=f32))
-        low, high, _ = PARTS[part]
-        ex_s[0, 8 + 8 * low : 8 + 8 * high, :] += product[:, 0:128]
-        ex_s[3, 8 + 8 * low : 8 + 8 * high, :] += product[:, 128:256]
     first = jnp.where(lax.broadcasted_iota(jnp.int32, (8, 512), 0) == 0, 1.0, 0.0)
     zero8 = jnp.zeros((8, 512), f32)
 
@@ -311,35 +328,34 @@
         at = pl.ds(pl.multiple_of(base * BLOCK, 512), 512)
         (cu, su), (cv, sv), (cw, sw) = (harmonics(rows[d]) for d in range(3))
 
-        def put(t, low_tile, high_tile):
+        def put(t, low_tile, high_tile, g):
             both = jnp.concatenate([low_tile, high_tile], 0)
             utab[8 * t : 8 * t + 16, at] = both
-            high, low = split(both)
-            first_row = 8 * (t + (0 if t < PARTS[1][0] else PARTS[1][0]))
-            ubf[first_row : first_row + 16, at] = high
-            first_row += 8 * (PARTS[0][1] if t < PARTS[1][0] else TILES - PARTS[1][0])
-            ubf[first_row : first_row + 16, at] = low.astype(bf16)
-
-        put(0, first, zero8)
-        put(2, cv, sv)
-        put(4, cu, su)
+            if g is not None:
+                put_split(gbf, g, at, both * rows[3])
+                put_split(gone, g, slice(None), both)
+
+        put(0, first, zero8, 0)
+        put(2, cv, sv, 2)
+        put(4, cu, su, 4)
         for a in range(8):
             for ta, u in ((0, cu), (1, su)):
                 here = u[a : a + 1, :]
-                put(core_tile(ta, 0, a), here * cv, here * sv)
+                put(core_tile(ta, 0, a), here * cv, here * sv, REST + 2 * (a - 1) + 2 * ta if a % 2 else None)
 
         w = jnp.concatenate([cw, first, sw, zero8], 0)
-        wtab[:, at] = w
         whi, wlo = split(w)
+        w3 = jnp.concatenate([w, w * cu[0:1, :], w * su[0:1, :]], 0)
+        wcol[at, :] = columns(w3).T.astype(bf16)
         wlo = wlo.astype(bf16)
         wst[0:32, at] = whi
         wst[32:64, at] = whi
         wst[64:96, at] = wlo
         wst[96:128, at] = jnp.zeros((32, 512), bf16)
-        qhi, qlo = split(w * rows[3])
-        qlo = qlo.astype(bf16)
         for part in range(2):
-            accumulate(part, ubf_rows(part), at, jnp.concatenate([qhi, qlo, qhi, qlo, whi, wlo, whi, wlo], 0))
+            mine = gbf_rows(part)
+            ex_s[0, ex_rows(part), :] += fold(jnp.dot(gbf[mine, at], wcol[at, :], preferred_element_type=f32))
+            ex_s[3, ex_rows(part), :] += fold(jnp.dot(gone[mine, :], wcol[at, :], preferred_element_type=f32))
         return carry
 
     lax.fori_loop(0, 4, arrive, 0)
@@ -350,7 +366,7 @@
     bond = buf[:, 6, :]
 
     def share(r, part):
-        low, high, _ = PARTS[part]
+        low, high = GPARTS[part]
         rows = pl.ds(0, 8 + 8 * high) if part == 0 else pl.ds(8 + 8 * low, 8 * (high - low))
         return pltpu.make_async_remote_copy(
             ex_s.at[r, rows],
@@ -362,7 +378,7 @@
         )
 
     def put_ends(r, weighted):
-        ex_s[r, 0:8, :] = jnp.concatenate(
+        ex_s[r, 0:8, 0:128] = jnp.concatenate(
             [weighted[0:1, :], weighted[15:16, :], bond[0:1, :], bond[15:16, :], jnp.zeros((4, 128), f32)], 0
         )
 
@@ -374,11 +390,30 @@
     number = jnp.where((lane16 & 15) < 8, (lane16 & 15) + 1, 0).astype(f32)
     slope = jnp.where((lane16 & 16) == 0, number, -number)
 
+    def tensor(r, part):
+        rows = ex_rows(part)
+        sums = ex_s[r, rows, :] + ex_r[r, rows, :]
+        plain, sines = sums[:, 0:128], sums[:, 128:256]
+        plain = plain + pltpu.roll(plain, 64, 1)
+        moved = pltpu.roll(plain, 32, 1)
+        even = (lax.broadcasted_iota(jnp.int32, plain.shape, 1) & 32) == 0
+        ones, cosines = jnp.where(even, plain, moved), jnp.where(even, moved, plain)
+        sines = sines + pltpu.roll(sines, 32, 1)
+        tiles = []
+        base = 0
+        if part == 0:
+            tiles += [ones[0 : 8 * REST, :], cosines[16:32, :], sines[16:32, :]]
+            base = REST
+        for n in range(base, rows.stop // 8 - rows.start // 8, 4):
+            both = slice(8 * n, 8 * n + 32)
+            c, s = slice(8 * n, 8 * n + 16), slice(8 * n + 16, 8 * n + 32)
+            tiles += [ones[both, :], cosines[c, :] - sines[s, :], cosines[s, :] + sines[c, :]]
+        size = 8 * (PARTS[part][1] - PARTS[part][0])
+        return jnp.concatenate(tiles, 0)[0:size, :]
+
     def mix(r, part, mean, slopes):
         low, high, numbers = PARTS[part]
-        rows = slice(8 + 8 * low, 8 + 8 * high)
-        total = ex_s[r, rows, :] + ex_r[r, rows, :]
-        total = total + pltpu.roll(total, 32, 1)
+        total = tensor(r, part)
         if r > 0:
             if part == 0:
                 mean = total[0:1, 8:9] * (1.0 / ATOMS)
@@ -461,23 +496,16 @@
         near_sums((0, SLOTS - 1), out)
 
     def refactor(r, values):
-        total = None
-        rows = ubf_rows(0)
-        for k in range(4):
-            for j in range(4 * k, 4 * k + 4):
+        for part in range(2):
+            for j in range(SLOTS):
                 at = slice(j * BLOCK, (j + 1) * BLOCK)
-                qhi, qlo = split(wtab[:, at] * values[j : j + 1, :])
-                qlo = qlo.astype(bf16)
-                acols[:, at] = jnp.concatenate([qhi, qlo, qhi, qlo], 0)
-            at = slice(512 * k, 512 * k + 512)
-            term = lax.dot_general(ubf[rows, at], acols[:, at], NT, preferred_element_type=f32)
-            total = term if total is None else total + term
-        ex_s[r, 8 : 8 + 8 * PARTS[0][1], :] = fold(0, total)
-        share(r, 0).start()
-        ex_s[r, 8 + 8 * PARTS[1][0] : EXROWS, :] = fold(
-            1, lax.dot_general(ubf[ubf_rows(1), :], acols[...], NT, preferred_element_type=f32)
-        )
-        share(r, 1).start()
+                row = values[j : j + 1, :]
+                for g in range(GPARTS[part][0], GPARTS[part][1], 2):
+                    n, ta = (g - REST) // 4, ((g - REST) // 2) % 2
+                    t = g if g < REST else core_tile(ta, 0, 2 * n + 1)
+                    put_split(gbf, g, at, utab[8 * t : 8 * t + 16, at] * row)
+            ex_s[r, ex_rows(part), :] = fold(jnp.dot(gbf[gbf_rows(part), :], wcol[...], preferred_element_type=f32))
+            share(r, part).start()
 
     def relax(charge, near):
         potential_here = ewald_scale * phi_s[...]
@@ -501,7 +529,7 @@
     share(0, 0).wait()
     mix(0, 0, None, False)
     potential(0)
-    ends = ex_r[0, 0:8, :]
+    ends = ex_r[0, 0:8, 0:128]
     outer_near(bond, ends[3:4, :], ends[2:3, :], nbond_s)
     outer_near(weighted, ends[1:2, :], ends[0:1, :], near_s)
     share(0, 1).wait()
@@ -509,8 +537,8 @@
     potential(1)
     relaxed = relax(charge, near_s[...])
     ones_share.wait()
-    weight_of_ones = ex_s[3, 8:EXROWS, :] + ex_r[3, 8:EXROWS, :]
-    gtab[...] = weight_of_ones + pltpu.roll(weight_of_ones, 32, 1)
+    for part in range(2):
+        gtab[8 * PARTS[part][0] : 8 * PARTS[part][1], :] = tensor(3, part)
 
     weighted = bond * relaxed
     put_ends(1, weighted)
@@ -519,7 +547,7 @@
     share(1, 0).wait()
     mean = mix(1, 0, None, False)
     potential(0)
-    ends = ex_r[1, 0:8, :]
+    ends = ex_r[1, 0:8, 0:128]
     outer_near(weighted, ends[1:2, :], ends[0:1, :], near_s)
     share(1, 1).wait()
     mix(1, 1, mean, False)
@@ -672,13 +700,13 @@
             pltpu.VMEM((SLOTS, 8, 128), f32),
             pltpu.VMEM((SLOTS, 8, 128), jnp.int32),
             pltpu.VMEM((ROWS, HALF), f32),
-            pltpu.VMEM((2 * ROWS, HALF), bf16),
-            pltpu.VMEM((32, HALF), f32),
-            pltpu.VMEM((128, HALF), bf16),
+            pltpu.VMEM((2 * GROWS, HALF), bf16),
+            pltpu.VMEM((2 * GROWS, 512), bf16),
+            pltpu.VMEM((HALF, 256), bf16),
             pltpu.VMEM((128, HALF), bf16),
             pltpu.VMEM((4, 96, 128), f32),
-            pltpu.VMEM((4, EXROWS, 128), f32),
-            pltpu.VMEM((4, EXROWS, 128), f32),
+            pltpu.VMEM((4, EXROWS, 256), f32),
+            pltpu.VMEM((4, EXROWS, 256), f32),
             pltpu.VMEM((3, 8, HALF), f32),
             pltpu.VMEM((ROWS, 128), f32),
             pltpu.VMEM((2 * ROWS, 128), bf16),

time: 30.4 us -> 29.9 us (0.984)
  Pallas kernels: 29.6 us -> 29.1 us
    pallas_call x1, Pallas kernels: 29 us -> 28.5 us  [step(): pl.pallas_call(kernel_body, out_shape=pltpu.VMEM((7, 4, BLOCK), f32), in_...]
where the time goes in v4:
time: 29.9 us; the launch traced here: 29.7 us
  Pallas kernels  29.1 us (97%)
  between operations  0.64 us (2%)
    pallas_call x1, Pallas kernels, step(): pl.pallas_call(kernel_body, out_shape=pltpu.VMEM((7, 4, BLOCK), f32), in_...  28.5 us
    pallas_call x1, Pallas kernels, step(): pl.pallas_call(emit_body, out_shape=(spatial, spatial, jax.ShapeDtypeStru...  0.63 us

profile of v4, /device:TPU:1, one launch (start us, length us, event | category | flops | bytes accessed | tf_op | source)
XLA Modules:
  0.0 29.7 jit_solution(6371818162620788003)
XLA Ops:
  0.6 28.5 %pimd_step.1.packed = f32[7,4,128]{2,1,0:T(4,128)S(1)} custom-call(f32[3,4,128]{2,1,0:T(4,128)} %bitcast.7, f32[3,4,128]{2,1,0:T(4,128)} %bitcast.8, f32[4,128]{1,0:T(4,128)} %chg_hbm.1, s32[1,128]{1,0:T(1,128)} %bitcast.9, s32[8,128]{1,0:T(8,128)} %nbr_hbm.1, s32[3,2048]{1,0:T(4,128)} %k_hbm.1, f32[1,2048]{1,0:T(1,128)} %bitcast.6, f32[8]{0:T(128)} %chi_hbm.1, ...), custom_call_target="tpu_custom_call" | custom-call | tf_op jit(solution)/shard_map/pimd_step/pallas_call | solution.py:685
  29.1 0.6 %emit.1 = (f32[3,4,128]{2,1,0:T(4,128)}, f32[3,4,128]{2,1,0:T(4,128)}, f32[4,128]{1,0:T(4,128)}) custom-call(f32[7,4,128]{2,1,0:T(4,128)S(1)} %pimd_step.1.packed), custom_call_target="tpu_custom_call" | custom-call | tf_op jit(solution)/shard_map/emit/pallas_call | solution.py:748

commit v5 on v4

--- a/solution.py
+++ b/solution.py
@@ -332,8 +332,8 @@
             both = jnp.concatenate([low_tile, high_tile], 0)
             utab[8 * t : 8 * t + 16, at] = both
             if g is not None:
-                put_split(gbf, g, at, both * rows[3])
-                put_split(gone, g, slice(None), both)
+                put_split(gone, g, slice(None), both * rows[3])
+                put_split(gone.at[2 * GROWS : 4 * GROWS], g, slice(None), both)
 
         put(0, first, zero8, 0)
         put(2, cv, sv, 2)
@@ -352,10 +352,11 @@
         wst[32:64, at] = whi
         wst[64:96, at] = wlo
         wst[96:128, at] = jnp.zeros((32, 512), bf16)
+        product = jnp.dot(gone[...], wcol[at, :], preferred_element_type=f32)
         for part in range(2):
             mine = gbf_rows(part)
-            ex_s[0, ex_rows(part), :] += fold(jnp.dot(gbf[mine, at], wcol[at, :], preferred_element_type=f32))
-            ex_s[3, ex_rows(part), :] += fold(jnp.dot(gone[mine, :], wcol[at, :], preferred_element_type=f32))
+            ex_s[0, ex_rows(part), :] += fold(product[mine, :])
+            ex_s[3, ex_rows(part), :] += fold(product[2 * GROWS + mine.start : 2 * GROWS + mine.stop, :])
         return carry
 
     lax.fori_loop(0, 4, arrive, 0)
@@ -455,20 +456,23 @@
     def potential(part):
         low, high, _ = PARTS[part]
         rows = slice(8 * low, 8 * high)
-        for i in range(SLOTS // 2):
-            at = slice(i * 256, i * 256 + 256)
-            fields = jnp.dot(lhs[rows, :], wst[:, at], preferred_element_type=f32)
-            sums = [None] * 4
-            for t in range(low, high):
-                term = tile(fields, t - low) * utab[8 * t : 8 * t + 8, at]
-                sums[t % 4] = term if sums[t % 4] is None else sums[t % 4] + term
-            total = (sums[0] + sums[1]) + (sums[2] + sums[3])
-            if part == 0:
-                acc[0, :, at] = total
-            else:
-                row = jnp.sum(total + acc[0, :, at], 0, keepdims=True)
-                phi_s[2 * i : 2 * i + 1, :] = row[:, 0:128]
-                phi_s[2 * i + 1 : 2 * i + 2, :] = row[:, 128:256]
+        for i in range(HALF // 2048):
+            whole = jnp.dot(lhs[rows, :], wst[:, i * 2048 : (i + 1) * 2048], preferred_element_type=f32)
+            for k in range(2048 // 256):
+                at = slice(i * 2048 + k * 256, i * 2048 + k * 256 + 256)
+                fields = whole[:, k * 256 : k * 256 + 256]
+                sums = [None] * 4
+                for t in range(low, high):
+                    term = tile(fields, t - low) * utab[8 * t : 8 * t + 8, at]
+                    sums[t % 4] = term if sums[t % 4] is None else sums[t % 4] + term
+                total = (sums[0] + sums[1]) + (sums[2] + sums[3])
+                if part == 0:
+                    acc[0, :, at] = total
+                else:
+                    row = jnp.sum(total + acc[0, :, at], 0, keepdims=True)
+                    j = (i * 2048 + k * 256) // 128
+                    phi_s[j : j + 1, :] = row[:, 0:128]
+                    phi_s[j + 1 : j + 2, :] = row[:, 128:256]
 
     lane_at = lax.broadcasted_iota(jnp.int32, (8, BLOCK), 1)
 
@@ -530,20 +534,20 @@
     mix(0, 0, None, False)
     potential(0)
     ends = ex_r[0, 0:8, 0:128]
-    outer_near(bond, ends[3:4, :], ends[2:3, :], nbond_s)
     outer_near(weighted, ends[1:2, :], ends[0:1, :], near_s)
     share(0, 1).wait()
     mix(0, 1, None, False)
     potential(1)
     relaxed = relax(charge, near_s[...])
-    ones_share.wait()
-    for part in range(2):
-        gtab[8 * PARTS[part][0] : 8 * PARTS[part][1], :] = tensor(3, part)
 
     weighted = bond * relaxed
     put_ends(1, weighted)
     refactor(1, relaxed)
     inner_near(weighted, near_s)
+    ones_share.wait()
+    for part in range(2):
+        gtab[8 * PARTS[part][0] : 8 * PARTS[part][1], :] = tensor(3, part)
+    outer_near(bond, ends[3:4, :], ends[2:3, :], nbond_s)
     share(1, 0).wait()
     mean = mix(1, 0, None, False)
     potential(0)
@@ -560,11 +564,41 @@
 
     ones = lax.broadcasted_iota(jnp.int32, (8, 256), 0).astype(f32) + 1.0
 
+    my_bead = 2 * x_lo + z % 2
+
+    def force_copy(k, m):
+        i = (z + 1 + k) % 2
+        home = core * 16 + (2 * quad + i) * 2 + m
+        return home, pltpu.make_async_remote_copy(
+            fsend.at[2 * k + m],
+            frecv.at[my_bead],
+            fs_sem.at[2 * k + m],
+            fr_sem.at[my_bead],
+            device_id={"atoms": home},
+            device_id_type=MESH,
+        )
+
+    def force_start(k):
+        for m in range(2):
+            home, copy = force_copy(k, m)
+            if k == 0:
+                copy.start()
+            else:
+
+                @pl.when(home != me)
+                def _():
+                    copy.start()
+
+                @pl.when(home == me)
+                def _():
+                    pltpu.make_async_copy(fsend.at[2 * k + m], frecv.at[my_bead], fr_sem.at[my_bead]).start()
+
     def force(part):
         low, high, numbers = PARTS[part]
-        for i in range(2):
+        for k in range(2):
+            i = (z + 1 + k) % 2
             at = pl.ds(pl.multiple_of(quad * 512 + i * 256, 256), 256)
-            keep = slice(i * 256, i * 256 + 256)
+            keep = slice(k * 256, k * 256 + 256)
             plain = jnp.dot(lhs[8 * low : 8 * high, :], wst[:, at], preferred_element_type=f32)
             sloped = jnp.dot(lhs[ROWS + 8 * low : ROWS + 8 * high, :], wst[:, at], preferred_element_type=f32)
             basis = {t: utab[8 * t : 8 * t + 8, at] for t in range(low, high)}
@@ -597,9 +631,10 @@
                 for m in range(2):
                     own = near_s[pl.ds(quad * 4 + 2 * i + m, 1), :]
                     piece = slice(128 * m, 128 * m + 128)
-                    fsend[2 * i + m] = jnp.concatenate(
+                    fsend[2 * k + m] = jnp.concatenate(
                         [dx[:, piece], dy[:, piece], dz[:, piece], own, jnp.zeros((4, 128), f32)], 0
                     )
+                force_start(k)
 
     share(2, 0).wait()
     mean = mix(2, 0, None, True)
@@ -608,25 +643,6 @@
     share(2, 1).wait()
     mix(2, 1, mean, True)
     force(1)
-
-    my_bead = 2 * x_lo + z % 2
-
-    def force_copy(m):
-        home = core * 16 + (2 * quad + (m >> 1)) * 2 + (m & 1)
-        return home, pltpu.make_async_remote_copy(
-            fsend.at[m], frecv.at[my_bead], fs_sem.at[m], fr_sem.at[my_bead], device_id={"atoms": home}, device_id_type=MESH
-        )
-
-    for m in range(4):
-        home, copy = force_copy(m)
-
-        @pl.when(home != me)
-        def _():
-            copy.start()
-
-        @pl.when(home == me)
-        def _():
-            pltpu.make_async_copy(fsend.at[m], frecv.at[my_bead], fr_sem.at[my_bead]).start()
 
     for make in (data_copy, nbr_copy):
         for b, o in order:
@@ -657,12 +673,16 @@
         speed = vel_s[d] + time_step * (ewald_force * inv_mass - spring_rate * laplace)
         out_ref[3 + d] = speed
         out_ref[d] = here + time_step * speed
-    for m in range(4):
-        home, copy = force_copy(m)
-
-        @pl.when(home != me)
-        def _():
-            copy.wait_send()
+    for k in range(2):
+        for m in range(2):
+            home, copy = force_copy(k, m)
+            if k == 0:
+                copy.wait_send()
+            else:
+
+                @pl.when(home != me)
+                def _():
+                    copy.wait_send()
 
 
 def emit_body(packed, npos_hbm, nvel_hbm, nchg_hbm, sems):
@@ -701,7 +721,7 @@
             pltpu.VMEM((SLOTS, 8, 128), jnp.int32),
             pltpu.VMEM((ROWS, HALF), f32),
             pltpu.VMEM((2 * GROWS, HALF), bf16),
-            pltpu.VMEM((2 * GROWS, 512), bf16),
+            pltpu.VMEM((4 * GROWS, 512), bf16),
             pltpu.VMEM((HALF, 256), bf16),
             pltpu.VMEM((128, HALF), bf16),
             pltpu.VMEM((4, 96, 128), f32),

time: 29.9 us -> 29.7 us (level)
  no operation moved by 1% of the time
where the time goes in v5:
time: 29.7 us; the launch traced here: 29.6 us
  Pallas kernels  28.9 us (97%)
  between operations  0.64 us (2%)
    pallas_call x1, Pallas kernels, step(): pl.pallas_call(kernel_body, out_shape=pltpu.VMEM((7, 4, BLOCK), f32), in_...  28.3 us
    pallas_call x1, Pallas kernels, step(): pl.pallas_call(emit_body, out_shape=(spatial, spatial, jax.ShapeDtypeStru...  0.63 us

profile of v5, /device:TPU:1, one launch (start us, length us, event | category | flops | bytes accessed | tf_op | source)
XLA Modules:
  0.0 29.6 jit_solution(5490573892743050366)
XLA Ops:
  0.6 28.3 %pimd_step.1.packed = f32[7,4,128]{2,1,0:T(4,128)S(1)} custom-call(f32[3,4,128]{2,1,0:T(4,128)} %bitcast.7, f32[3,4,128]{2,1,0:T(4,128)} %bitcast.8, f32[4,128]{1,0:T(4,128)} %chg_hbm.1, s32[1,128]{1,0:T(1,128)} %bitcast.9, s32[8,128]{1,0:T(8,128)} %nbr_hbm.1, s32[3,2048]{1,0:T(4,128)} %k_hbm.1, f32[1,2048]{1,0:T(1,128)} %bitcast.6, f32[8]{0:T(128)} %chi_hbm.1, ...), custom_call_target="tpu_custom_call" | custom-call | tf_op jit(solution)/shard_map/pimd_step/pallas_call | solution.py:705
  29.0 0.6 %emit.1 = (f32[3,4,128]{2,1,0:T(4,128)}, f32[3,4,128]{2,1,0:T(4,128)}, f32[4,128]{1,0:T(4,128)}) custom-call(f32[7,4,128]{2,1,0:T(4,128)S(1)} %pimd_step.1.packed), custom_call_target="tpu_custom_call" | custom-call | tf_op jit(solution)/shard_map/emit/pallas_call | solution.py:768

commit v6 on v5

--- a/solution.py
+++ b/solution.py
@@ -417,7 +417,8 @@
         total = tensor(r, part)
         if r > 0:
             if part == 0:
-                mean = total[0:1, 8:9] * (1.0 / ATOMS)
+                whole = ex_s[r, 8:9, 0:128] + ex_r[r, 8:9, 0:128]
+                mean = (whole[:, 8:9] + whole[:, 72:73]) * (1.0 / ATOMS)
             total = total - mean * gtab[8 * low : 8 * high, :]
         swapped = flip(total)
 

time: 29.7 us -> 29.6 us (level)
  no operation moved by 1% of the time
where the time goes in v6:
time: 29.6 us; the launch traced here: 29.5 us
  Pallas kernels  28.8 us (97%)
  between operations  0.64 us (2%)
    pallas_call x1, Pallas kernels, step(): pl.pallas_call(kernel_body, out_shape=pltpu.VMEM((7, 4, BLOCK), f32), in_...  28.2 us
    pallas_call x1, Pallas kernels, step(): pl.pallas_call(emit_body, out_shape=(spatial, spatial, jax.ShapeDtypeStru...  0.63 us

profile of v6, /device:TPU:1, one launch (start us, length us, event | category | flops | bytes accessed | tf_op | source)
XLA Modules:
  0.0 29.5 jit_solution(10572771770407471733)
XLA Ops:
  0.6 28.2 %pimd_step.1.packed = f32[7,4,128]{2,1,0:T(4,128)S(1)} custom-call(f32[3,4,128]{2,1,0:T(4,128)} %bitcast.7, f32[3,4,128]{2,1,0:T(4,128)} %bitcast.8, f32[4,128]{1,0:T(4,128)} %chg_hbm.1, s32[1,128]{1,0:T(1,128)} %bitcast.9, s32[8,128]{1,0:T(8,128)} %nbr_hbm.1, s32[3,2048]{1,0:T(4,128)} %k_hbm.1, f32[1,2048]{1,0:T(1,128)} %bitcast.6, f32[8]{0:T(128)} %chi_hbm.1, ...), custom_call_target="tpu_custom_call" | custom-call | tf_op jit(solution)/shard_map/pimd_step/pallas_call | solution.py:706
  28.9 0.6 %emit.1 = (f32[3,4,128]{2,1,0:T(4,128)}, f32[3,4,128]{2,1,0:T(4,128)}, f32[4,128]{1,0:T(4,128)}) custom-call(f32[7,4,128]{2,1,0:T(4,128)S(1)} %pimd_step.1.packed), custom_call_target="tpu_custom_call" | custom-call | tf_op jit(solution)/shard_map/emit/pallas_call | solution.py:769

commit v7 on v6

--- a/solution.py
+++ b/solution.py
@@ -658,7 +658,13 @@
 
     to_next.wait()
     to_prev.wait()
-    inv_mass = 1.0 / mass_row
+    gain = (-two_pi * ewald_scale * time_step) / mass_row
+    drift = []
+    for d in range(3):
+        here = pos_s[d]
+        before = jnp.concatenate([halo[0, d : d + 1, :], here[0:3, :]], 0)
+        after = jnp.concatenate([here[1:4, :], halo[1, d : d + 1, :]], 0)
+        drift.append(vel_s[d] - (time_step * spring_rate) * (2.0 * here - before - after))
     for b in range(4):
         pltpu.make_async_remote_copy(
             fsend.at[0], frecv.at[b], fs_sem.at[0], fr_sem.at[b], device_id={"atoms": partner}, device_id_type=MESH
@@ -666,12 +672,8 @@
     charges = frecv[:, 3, :]
     out_ref[6] = charges
     for d in range(3):
-        ewald_force = (-two_pi * ewald_scale) * charges * frecv[:, d, :]
         here = pos_s[d]
-        before = jnp.concatenate([halo[0, d : d + 1, :], here[0:3, :]], 0)
-        after = jnp.concatenate([here[1:4, :], halo[1, d : d + 1, :]], 0)
-        laplace = 2.0 * here - before - after
-        speed = vel_s[d] + time_step * (ewald_force * inv_mass - spring_rate * laplace)
+        speed = drift[d] + gain * charges * frecv[:, d, :]
         out_ref[3 + d] = speed
         out_ref[d] = here + time_step * speed
     for k in range(2):

time: 29.6 us -> 29.6 us (level)
  no operation moved by 1% of the time
where the time goes in v7:
time: 29.6 us; the launch traced here: 29.5 us
  Pallas kernels  28.8 us (97%)
  between operations  0.64 us (2%)
    pallas_call x1, Pallas kernels, step(): pl.pallas_call(kernel_body, out_shape=pltpu.VMEM((7, 4, BLOCK), f32), in_...  28.2 us
    pallas_call x1, Pallas kernels, step(): pl.pallas_call(emit_body, out_shape=(spatial, spatial, jax.ShapeDtypeStru...  0.63 us

profile of v7, /device:TPU:1, one launch (start us, length us, event | category | flops | bytes accessed | tf_op | source)
XLA Modules:
  0.0 29.5 jit_solution(1010529804849842434)
XLA Ops:
  0.6 28.2 %pimd_step.1.packed = f32[7,4,128]{2,1,0:T(4,128)S(1)} custom-call(f32[3,4,128]{2,1,0:T(4,128)} %bitcast.7, f32[3,4,128]{2,1,0:T(4,128)} %bitcast.8, f32[4,128]{1,0:T(4,128)} %chg_hbm.1, s32[1,128]{1,0:T(1,128)} %bitcast.9, s32[8,128]{1,0:T(8,128)} %nbr_hbm.1, s32[3,2048]{1,0:T(4,128)} %k_hbm.1, f32[1,2048]{1,0:T(1,128)} %bitcast.6, f32[8]{0:T(128)} %chi_hbm.1, ...), custom_call_target="tpu_custom_call" | custom-call | tf_op jit(solution)/shard_map/pimd_step/pallas_call | solution.py:708
  28.8 0.6 %emit.1 = (f32[3,4,128]{2,1,0:T(4,128)}, f32[3,4,128]{2,1,0:T(4,128)}, f32[4,128]{1,0:T(4,128)}) custom-call(f32[7,4,128]{2,1,0:T(4,128)S(1)} %pimd_step.1.packed), custom_call_target="tpu_custom_call" | custom-call | tf_op jit(solution)/shard_map/emit/pallas_call | solution.py:771
